TPU v7x, 256 devices: a whole 4x4x8 slice. The times are simulated.
256 devices in a mesh: harm: 8 (over x, y_lo), dom: 32 (over y_hi, z, core).
Axes of the slice: x: 4, y: 4 (y_hi: 2, y_lo: 2; y = y_hi * 2 + y_lo), z: 8, core: 2. Of those that a mesh axis runs over, the one named last changes fastest.
Arguments:
- response: float32 [2, 64, 64, 8192], P(None, 'harm', None, 'dom'), may hold values from -6 to 6
- base_coeff: float32 [2, 17, 64, 8192], P(None, None, None, 'dom'), may hold values from -1.5 to 1.5
- volume_mat: float32 [64, 64], replicated, may hold values from -0.75 to 0.75
- trace_mats: float32 [4, 16, 64], replicated, may hold values from -0.75 to 0.75
- lift_mat: float32 [64, 16], replicated, may hold values from -1.5 to 1.5
- round_masks: int32 [4], replicated, may hold values from 1 to 31, as said below
- send_elem: int32 [4, 2048], P(None, 'dom'), may hold values from 0 to 255
- send_face: int32 [4, 2048], P(None, 'dom'), may hold values from 0 to 3
- recv_elem: int32 [4, 2048], P(None, 'dom'), may hold values from 0 to 255
Outputs:
- image: float32 [2, 64, 64, 8192], P(None, 'harm', None, 'dom')
Inputs may be any that keep to these rules, and one draw needn't show every extreme that they name: `round_masks`: 4 distinct masks, among them the smallest and the largest possible mask; in each round partition p is matched with partition p XOR mask.
All inputs are finite; a program needn't handle non-finite values.
Results may differ from a plain program's by a relative error of at most 0.0001.
Values sent between devices are 32-bit elements; how exact they have to be, the bound alone decides.
No kernel may reach another device: no remote copies, remote signals or barrier semaphores. Data moves between devices by JAX's collectives and lax.ppermute only.
A program may use at most 64 MiB of HBM per device.

v0:
```python
import jax
import jax.numpy as jnp
from jax import lax
from jax.sharding import PartitionSpec as P

REACH = 8
ROUNDS = 4


base_omega = 0.2


def padded(block, sides, width):
    for axis, dim in sides:
        count = lax.axis_size(axis)
        forward = [(i, i + 1) for i in range(count - 1)]
        forward.append((count - 1, 0))
        backward = [(target, source) for source, target in forward]
        low = lax.ppermute(
            lax.slice_in_dim(block, block.shape[dim] - width, None, axis=dim), axis, forward
        )
        high = lax.ppermute(lax.slice_in_dim(block, 0, width, axis=dim), axis, backward)
        block = jnp.concatenate([low, block, high], axis=dim)
    return block


def from_partner(value, axis, bit):
    return lax.ppermute(value, axis, [(i, i ^ 1 << bit) for i in range(lax.axis_size(axis))])


def convolve_window(window, coeff, harm_count):
    real_acc = jnp.zeros((harm_count,) + window.shape[2:], jnp.float32)
    imag_acc = jnp.zeros((harm_count,) + window.shape[2:], jnp.float32)
    for offset in range(-REACH, REACH + 1):
        shifted = window[:, REACH - offset : REACH - offset + harm_count]
        c_real = coeff[0, offset + REACH][None]
        c_imag = coeff[1, offset + REACH][None]
        real_acc = real_acc + c_real * shifted[0] - c_imag * shifted[1]
        imag_acc = imag_acc + c_real * shifted[1] + c_imag * shifted[0]
    return jnp.stack([real_acc, imag_acc])


def face_select(trace_mats, faces):
    select = jnp.zeros(faces.shape + trace_mats.shape[1:], jnp.float32)
    for face_id in range(4):
        select = select + jnp.where((faces == face_id)[..., None, None], trace_mats[face_id], 0.0)
    return select


def local(
    response,
    base_coeff,
    volume_mat,
    trace_mats,
    lift_mat,
    round_masks,
    send_elem,
    send_face,
    recv_elem,
):
    harm_count = response.shape[1]
    group_count = lax.axis_size("harm")
    window = padded(response, (("harm", 1),), REACH)
    conv = convolve_window(window, base_coeff, harm_count)
    period = harm_count * group_count
    slot_ids = lax.axis_index("harm") * harm_count + jnp.arange(harm_count, dtype=jnp.int32)
    wave_number = jnp.where(slot_ids < period // 2, slot_ids, slot_ids - period).astype(jnp.float32)
    frequency = base_omega * wave_number[:, None, None]
    derived = jnp.einsum("ab,cjbe->cjae", volume_mat, conv, precision=lax.Precision.HIGHEST)
    image = jnp.stack([derived[0] - frequency * response[1], derived[1] + frequency * response[0]])
    traces = []
    for step_round in range(ROUNDS):
        picked = jnp.take(response, send_elem[step_round], axis=3)
        select = face_select(trace_mats, send_face[step_round])
        traces.append(jnp.einsum("sgb,cjbs->cjgs", select, picked, precision=lax.Precision.HIGHEST))
    num_parts = lax.axis_size("dom")
    bit_count = num_parts.bit_length() - 1
    received = []
    for step_round in range(ROUNDS):
        moving = traces[step_round]
        for bit_pos in range(bit_count):
            swapped = from_partner(moving, "dom", bit_pos)
            bit_set = jnp.bitwise_and(jnp.right_shift(round_masks[step_round], bit_pos), 1)
            moving = jnp.where(bit_set == 1, swapped, moving)
        received.append(moving)
    for step_round in range(ROUNDS):
        lifted = jnp.einsum(
            "bg,cjgs->cjbs", lift_mat, received[step_round], precision=lax.Precision.HIGHEST
        )
        image = image.at[:, :, :, recv_elem[step_round]].add(lifted)
    return image


def solution(mesh):
    in_specs = (
        P(None, "harm", None, "dom"),
        P(None, None, None, "dom"),
        P(),
        P(),
        P(),
        P(),
        P(None, "dom"),
        P(None, "dom"),
        P(None, "dom"),
    )
    out_specs = P(None, "harm", None, "dom")
    return jax.shard_map(local, mesh=mesh, in_specs=in_specs, out_specs=out_specs, check_vma=False)
```

profile of v0, /device:TPU:96, one launch (start us, length us, event | category | flops | bytes accessed | tf_op | source)
XLA Modules:
  0.0 371.7 jit_solution(12503226350234945483)
XLA Ops:
  4.2 3.2 copy.24
  38.4 3.0 gather_fusion.3
  50.4 10.2 %collective-permute-done.3 = f32[2,8,16,64]{2,1,0,3:T(8,128)S(1)} collective-permute-done((f32[2,8,16,64]{2,1,0,3:T(8,128)S(1)}, f32[2,8,16,64]{2,1,0,3:T(8,128)S(1)}, u32[]{:S(2)}, u32[]{:S(2)}) %collective-permute-start.3) | collective-permute-done | bytes 65568 | tf_op jit(solution)/shard_map/ppermute | solution.py:28
  60.7 11.1 %collective-permute-done.8 = f32[2,8,16,64]{2,1,0,3:T(8,128)S(1)} collective-permute-done((f32[2,8,16,64]{2,1,0,3:T(8,128)S(1)}, f32[2,8,16,64]{2,1,0,3:T(8,128)S(1)}, u32[]{:S(2)}, u32[]{:S(2)}) %collective-permute-start.8) | collective-permute-done | bytes 65568 | tf_op jit(solution)/shard_map/ppermute | solution.py:28
  71.9 22.4 %collective-permute-done.13 = f32[2,8,16,64]{2,1,0,3:T(8,128)S(1)} collective-permute-done((f32[2,8,16,64]{2,1,0,3:T(8,128)S(1)}, f32[2,8,16,64]{2,1,0,3:T(8,128)S(1)}, u32[]{:S(2)}, u32[]{:S(2)}) %collective-permute-start.13) | collective-permute-done | bytes 65568 | tf_op jit(solution)/shard_map/ppermute | solution.py:28
  94.3 10.3 %collective-permute-done.18 = f32[2,8,16,64]{2,1,0,3:T(8,128)S(1)} collective-permute-done((f32[2,8,16,64]{2,1,0,3:T(8,128)S(1)}, f32[2,8,16,64]{2,1,0,3:T(8,128)S(1)}, u32[]{:S(2)}, u32[]{:S(2)}) %collective-permute-start.18) | collective-permute-done | bytes 65568 | tf_op jit(solution)/shard_map/ppermute | solution.py:28
  104.7 3.0 collective-permute-start.19
  107.8 40.9 %collective-permute-done.9 = f32[2,8,16,64]{2,1,0,3:T(8,128)S(1)} collective-permute-done((f32[2,8,16,64]{2,1,0,3:T(8,128)S(1)}, f32[2,8,16,64]{2,1,0,3:T(8,128)S(1)}, u32[]{:S(2)}, u32[]{:S(2)}) %collective-permute-start.9) | collective-permute-done | bytes 65568 | tf_op jit(solution)/shard_map/ppermute | solution.py:28
  148.8 6.2 %collective-permute-start.5 = (f32[2,8,16,64]{2,1,0,3:T(8,128)S(1)}, f32[2,8,16,64]{2,1,0,3:T(8,128)S(1)}, u32[]{:S(2)}, u32[]{:S(2)}) collective-permute-start(f32[2,8,16,64]{2,1,0,3:T(8,128)S(1)} %broadcast_select_fusion.17), channel_id=1, source_target_pairs={{0,8},{1,9},{2,10},{3,11},{4,12},{5,13},{6,14},{7,15},{8,0},{9,1},... | collective-permute-start | bytes 196616 | tf_op jit(solution)/shard_map/ppermute | solution.py:28
  155.0 16.4 %collective-permute-done.14 = f32[2,8,16,64]{2,1,0,3:T(8,128)S(1)} collective-permute-done((f32[2,8,16,64]{2,1,0,3:T(8,128)S(1)}, f32[2,8,16,64]{2,1,0,3:T(8,128)S(1)}, u32[]{:S(2)}, u32[]{:S(2)}) %collective-permute-start.14) | collective-permute-done | bytes 65568 | tf_op jit(solution)/shard_map/ppermute | solution.py:28
  171.5 6.3 %collective-permute-start.10 = (f32[2,8,16,64]{2,1,0,3:T(8,128)S(1)}, f32[2,8,16,64]{2,1,0,3:T(8,128)S(1)}, u32[]{:S(2)}, u32[]{:S(2)}) collective-permute-start(f32[2,8,16,64]{2,1,0,3:T(8,128)S(1)} %broadcast_select_fusion.12), channel_id=1, source_target_pairs={{0,8},{1,9},{2,10},{3,11},{4,12},{5,13},{6,14},{7,15},{8,0},{9,1},... | collective-permute-start | bytes 196616 | tf_op jit(solution)/shard_map/ppermute | solution.py:28
  177.8 16.2 %collective-permute-done.19 = f32[2,8,16,64]{2,1,0,3:T(8,128)S(1)} collective-permute-done((f32[2,8,16,64]{2,1,0,3:T(8,128)S(1)}, f32[2,8,16,64]{2,1,0,3:T(8,128)S(1)}, u32[]{:S(2)}, u32[]{:S(2)}) %collective-permute-start.19) | collective-permute-done | bytes 65568 | tf_op jit(solution)/shard_map/ppermute | solution.py:28
  194.0 73.3 %collective-permute-start.15 = (f32[2,8,16,64]{2,1,0,3:T(8,128)S(1)}, f32[2,8,16,64]{2,1,0,3:T(8,128)S(1)}, u32[]{:S(2)}, u32[]{:S(2)}) collective-permute-start(f32[2,8,16,64]{2,1,0,3:T(8,128)S(1)} %broadcast_select_fusion.7), channel_id=1, source_target_pairs={{0,8},{1,9},{2,10},{3,11},{4,12},{5,13},{6,14},{7,15},{8,0},{9,1},... | collective-permute-start | bytes 196616 | tf_op jit(solution)/shard_map/ppermute | solution.py:28
  267.5 3.3 collective-permute-start.6
  270.9 25.6 %collective-permute-done.15 = f32[2,8,16,64]{2,1,0,3:T(8,128)S(1)} collective-permute-done((f32[2,8,16,64]{2,1,0,3:T(8,128)S(1)}, f32[2,8,16,64]{2,1,0,3:T(8,128)S(1)}, u32[]{:S(2)}, u32[]{:S(2)}) %collective-permute-start.15) | collective-permute-done | bytes 65568 | tf_op jit(solution)/shard_map/ppermute | solution.py:28
  296.5 3.2 collective-permute-start.11
  299.8 13.7 %collective-permute-done.20 = f32[2,8,16,64]{2,1,0,3:T(8,128)S(1)} collective-permute-done((f32[2,8,16,64]{2,1,0,3:T(8,128)S(1)}, f32[2,8,16,64]{2,1,0,3:T(8,128)S(1)}, u32[]{:S(2)}, u32[]{:S(2)}) %collective-permute-start.20) | collective-permute-done | bytes 65568 | tf_op jit(solution)/shard_map/ppermute | solution.py:28
  313.4 3.2 collective-permute-start.16
  318.6 11.1 %collective-permute-done.16 = f32[2,8,16,64]{2,1,0,3:T(8,128)S(1)} collective-permute-done((f32[2,8,16,64]{2,1,0,3:T(8,128)S(1)}, f32[2,8,16,64]{2,1,0,3:T(8,128)S(1)}, u32[]{:S(2)}, u32[]{:S(2)}) %collective-permute-start.16) | collective-permute-done | bytes 65568 | tf_op jit(solution)/shard_map/ppermute | solution.py:28
  333.8 5.6 %collective-permute-done.21 = f32[2,8,16,64]{2,1,0,3:T(8,128)S(1)} collective-permute-done((f32[2,8,16,64]{2,1,0,3:T(8,128)S(1)}, f32[2,8,16,64]{2,1,0,3:T(8,128)S(1)}, u32[]{:S(2)}, u32[]{:S(2)}) %collective-permute-start.21) | collective-permute-done | bytes 65568 | tf_op jit(solution)/shard_map/ppermute | solution.py:28
  350.3 6.3 %scatter_fusion = f32[2,8,64,256]{2,1,3,0:T(8,128)S(1)} fusion(f32[2,8,64,256]{2,1,3,0:T(8,128)S(1)} %copy.26, s32[64]{0:T(128)S(1)} %copy-done.21, f32[64,2,8,64]{3,2,1,0:T(8,128)} %copy.27), kind=kCustom, calls=%fused_computation.4 | custom fusion | flops 65536 | bytes 786688 | tf_op jit(solution)/shard_map/scatter-add | solution.py:90
  356.6 6.3 %scatter_fusion.1 = f32[2,8,64,256]{2,1,3,0:T(8,128)S(1)} fusion(f32[2,8,64,256]{2,1,3,0:T(8,128)S(1)} %scatter_fusion, s32[64]{0:T(128)S(1)} %get-tuple-element.79, f32[64,2,8,64]{3,2,1,0:T(8,128)} %copy.30), kind=kCustom, calls=%fused_computation.5 | custom fusion | flops 65536 | bytes 786688 | tf_op jit(solution)/shard_map/scatter-add | solution.py:90
  362.9 3.6 scatter_fusion.2
  366.5 3.6 scatter_fusion.3
  (133 shorter events, 51.4 us)
Async XLA Ops:
  0.0 348.1 %copy-start = (f32[64,64]{1,0:T(8,128)S(1)}, f32[64,64]{1,0:T(8,128)}, u32[]{:S(2)}) copy-start(f32[64,64]{1,0:T(8,128)} %param.13) | copy-start | bytes 49156
  0.0 341.2 %collective-permute-start.1 = (f32[2,8,64,256]{3,2,1,0:T(8,128)}, f32[2,8,64,256]{3,2,1,0:T(8,128)S(1)}, u32[]{:S(2)}, u32[]{:S(2)}) collective-permute-start(f32[2,8,64,256]{3,2,1,0:T(8,128)} %param.11), channel_id=1, source_target_pairs={{0,32},{32,64},{64,96},{96,128},{128,160},{160,192},{192,224},{224... | collective-permute-start | bytes 3145736 | tf_op jit(solution)/shard_map/ppermute | solution.py:19
  1.7 340.1 %collective-permute-start = (f32[2,8,64,256]{3,2,1,0:T(8,128)}, f32[2,8,64,256]{3,2,1,0:T(8,128)S(1)}, u32[]{:S(2)}, u32[]{:S(2)}) collective-permute-start(f32[2,8,64,256]{3,2,1,0:T(8,128)} %param.11), channel_id=1, source_target_pairs={{32,0},{64,32},{96,64},{128,96},{160,128},{192,160},{224,192},{0,2... | collective-permute-start | bytes 3145736 | tf_op jit(solution)/shard_map/ppermute | solution.py:22
  13.1 30.8 %collective-permute-start.2 = (f32[2,8,16,64]{2,1,0,3:T(8,128)}, f32[2,8,16,64]{2,1,0,3:T(8,128)}, u32[]{:S(2)}, u32[]{:S(2)}) collective-permute-start(f32[2,8,16,64]{2,1,0,3:T(8,128)} %convolution_bitcast_fusion.8), channel_id=1, source_target_pairs={{0,1},{1,0},{2,3},{3,2},{4,5},{5,4},{6,7},{7,6},{8,9},{9,8},{10,11... | collective-permute-start | bytes 196616 | tf_op jit(solution)/shard_map/ppermute | solution.py:28
  17.5 28.1 %collective-permute-start.7 = (f32[2,8,16,64]{2,1,0,3:T(8,128)}, f32[2,8,16,64]{2,1,0,3:T(8,128)}, u32[]{:S(2)}, u32[]{:S(2)}) collective-permute-start(f32[2,8,16,64]{2,1,0,3:T(8,128)} %convolution_bitcast_fusion.7), channel_id=1, source_target_pairs={{0,1},{1,0},{2,3},{3,2},{4,5},{5,4},{6,7},{7,6},{8,9},{9,8},{10,11... | collective-permute-start | bytes 196616 | tf_op jit(solution)/shard_map/ppermute | solution.py:28
  22.5 24.5 %collective-permute-start.12 = (f32[2,8,16,64]{2,1,0,3:T(8,128)}, f32[2,8,16,64]{2,1,0,3:T(8,128)}, u32[]{:S(2)}, u32[]{:S(2)}) collective-permute-start(f32[2,8,16,64]{2,1,0,3:T(8,128)} %convolution_bitcast_fusion.6), channel_id=1, source_target_pairs={{0,1},{1,0},{2,3},{3,2},{4,5},{5,4},{6,7},{7,6},{8,9},{9,8},{10,11... | collective-permute-start | bytes 196616 | tf_op jit(solution)/shard_map/ppermute | solution.py:28
  44.0 6.1 %collective-permute-start.17 = (f32[2,8,16,64]{2,1,0,3:T(8,128)S(1)}, f32[2,8,16,64]{2,1,0,3:T(8,128)S(1)}, u32[]{:S(2)}, u32[]{:S(2)}) collective-permute-start(f32[2,8,16,64]{2,1,0,3:T(8,128)S(1)} %convolution_bitcast_fusion.5), channel_id=1, source_target_pairs={{0,1},{1,0},{2,3},{3,2},{4,5},{5,4},{6,7},{7,6},{8,9},{9,8},{10,11... | collective-permute-start | bytes 196616 | tf_op jit(solution)/shard_map/ppermute | solution.py:28
  45.7 14.9 %collective-permute-start.3 = (f32[2,8,16,64]{2,1,0,3:T(8,128)S(1)}, f32[2,8,16,64]{2,1,0,3:T(8,128)S(1)}, u32[]{:S(2)}, u32[]{:S(2)}) collective-permute-start(f32[2,8,16,64]{2,1,0,3:T(8,128)S(1)} %broadcast_select_fusion.15), channel_id=1, source_target_pairs={{0,2},{1,3},{2,0},{3,1},{4,6},{5,7},{6,4},{7,5},{8,10},{9,11},{10,... | collective-permute-start | bytes 196616 | tf_op jit(solution)/shard_map/ppermute | solution.py:28
  47.0 24.8 %collective-permute-start.8 = (f32[2,8,16,64]{2,1,0,3:T(8,128)S(1)}, f32[2,8,16,64]{2,1,0,3:T(8,128)S(1)}, u32[]{:S(2)}, u32[]{:S(2)}) collective-permute-start(f32[2,8,16,64]{2,1,0,3:T(8,128)S(1)} %broadcast_select_fusion.10), channel_id=1, source_target_pairs={{0,2},{1,3},{2,0},{3,1},{4,6},{5,7},{6,4},{7,5},{8,10},{9,11},{10,... | collective-permute-start | bytes 196616 | tf_op jit(solution)/shard_map/ppermute | solution.py:28
  50.1 44.1 %collective-permute-start.13 = (f32[2,8,16,64]{2,1,0,3:T(8,128)S(1)}, f32[2,8,16,64]{2,1,0,3:T(8,128)S(1)}, u32[]{:S(2)}, u32[]{:S(2)}) collective-permute-start(f32[2,8,16,64]{2,1,0,3:T(8,128)S(1)} %broadcast_select_fusion.5), channel_id=1, source_target_pairs={{0,2},{1,3},{2,0},{3,1},{4,6},{5,7},{6,4},{7,5},{8,10},{9,11},{10,... | collective-permute-start | bytes 196616 | tf_op jit(solution)/shard_map/ppermute | solution.py:28
  60.6 44.1 %collective-permute-start.18 = (f32[2,8,16,64]{2,1,0,3:T(8,128)S(1)}, f32[2,8,16,64]{2,1,0,3:T(8,128)S(1)}, u32[]{:S(2)}, u32[]{:S(2)}) collective-permute-start(f32[2,8,16,64]{2,1,0,3:T(8,128)S(1)} %broadcast_select_fusion), channel_id=1, source_target_pairs={{0,2},{1,3},{2,0},{3,1},{4,6},{5,7},{6,4},{7,5},{8,10},{9,11},{10,... | collective-permute-start | bytes 196616 | tf_op jit(solution)/shard_map/ppermute | solution.py:28
  71.8 32.9 %collective-permute-start.4 = (f32[2,8,16,64]{2,1,0,3:T(8,128)S(1)}, f32[2,8,16,64]{2,1,0,3:T(8,128)S(1)}, u32[]{:S(2)}, u32[]{:S(2)}) collective-permute-start(f32[2,8,16,64]{2,1,0,3:T(8,128)S(1)} %broadcast_select_fusion.16), channel_id=1, source_target_pairs={{0,4},{1,5},{2,6},{3,7},{4,0},{5,1},{6,2},{7,3},{8,12},{9,13},{10,... | collective-permute-start | bytes 196616 | tf_op jit(solution)/shard_map/ppermute | solution.py:28
  94.3 54.5 %collective-permute-start.9 = (f32[2,8,16,64]{2,1,0,3:T(8,128)S(1)}, f32[2,8,16,64]{2,1,0,3:T(8,128)S(1)}, u32[]{:S(2)}, u32[]{:S(2)}) collective-permute-start(f32[2,8,16,64]{2,1,0,3:T(8,128)S(1)} %broadcast_select_fusion.11), channel_id=1, source_target_pairs={{0,4},{1,5},{2,6},{3,7},{4,0},{5,1},{6,2},{7,3},{8,12},{9,13},{10,... | collective-permute-start | bytes 196616 | tf_op jit(solution)/shard_map/ppermute | solution.py:28
  104.7 66.8 %collective-permute-start.14 = (f32[2,8,16,64]{2,1,0,3:T(8,128)S(1)}, f32[2,8,16,64]{2,1,0,3:T(8,128)S(1)}, u32[]{:S(2)}, u32[]{:S(2)}) collective-permute-start(f32[2,8,16,64]{2,1,0,3:T(8,128)S(1)} %broadcast_select_fusion.6), channel_id=1, source_target_pairs={{0,4},{1,5},{2,6},{3,7},{4,0},{5,1},{6,2},{7,3},{8,12},{9,13},{10,... | collective-permute-start | bytes 196616 | tf_op jit(solution)/shard_map/ppermute | solution.py:28
  104.7 89.3 %collective-permute-start.19 = (f32[2,8,16,64]{2,1,0,3:T(8,128)S(1)}, f32[2,8,16,64]{2,1,0,3:T(8,128)S(1)}, u32[]{:S(2)}, u32[]{:S(2)}) collective-permute-start(f32[2,8,16,64]{2,1,0,3:T(8,128)S(1)} %broadcast_select_fusion.1), channel_id=1, source_target_pairs={{0,4},{1,5},{2,6},{3,7},{4,0},{5,1},{6,2},{7,3},{8,12},{9,13},{10,... | collective-permute-start | bytes 196616 | tf_op jit(solution)/shard_map/ppermute | solution.py:28
  148.8 118.6 %collective-permute-start.5 = (f32[2,8,16,64]{2,1,0,3:T(8,128)S(1)}, f32[2,8,16,64]{2,1,0,3:T(8,128)S(1)}, u32[]{:S(2)}, u32[]{:S(2)}) collective-permute-start(f32[2,8,16,64]{2,1,0,3:T(8,128)S(1)} %broadcast_select_fusion.17), channel_id=1, source_target_pairs={{0,8},{1,9},{2,10},{3,11},{4,12},{5,13},{6,14},{7,15},{8,0},{9,1},... | collective-permute-start | bytes 196616 | tf_op jit(solution)/shard_map/ppermute | solution.py:28
  171.5 96.1 %collective-permute-start.10 = (f32[2,8,16,64]{2,1,0,3:T(8,128)S(1)}, f32[2,8,16,64]{2,1,0,3:T(8,128)S(1)}, u32[]{:S(2)}, u32[]{:S(2)}) collective-permute-start(f32[2,8,16,64]{2,1,0,3:T(8,128)S(1)} %broadcast_select_fusion.12), channel_id=1, source_target_pairs={{0,8},{1,9},{2,10},{3,11},{4,12},{5,13},{6,14},{7,15},{8,0},{9,1},... | collective-permute-start | bytes 196616 | tf_op jit(solution)/shard_map/ppermute | solution.py:28
  194.0 102.5 %collective-permute-start.15 = (f32[2,8,16,64]{2,1,0,3:T(8,128)S(1)}, f32[2,8,16,64]{2,1,0,3:T(8,128)S(1)}, u32[]{:S(2)}, u32[]{:S(2)}) collective-permute-start(f32[2,8,16,64]{2,1,0,3:T(8,128)S(1)} %broadcast_select_fusion.7), channel_id=1, source_target_pairs={{0,8},{1,9},{2,10},{3,11},{4,12},{5,13},{6,14},{7,15},{8,0},{9,1},... | collective-permute-start | bytes 196616 | tf_op jit(solution)/shard_map/ppermute | solution.py:28
  267.4 46.1 %collective-permute-start.20 = (f32[2,8,16,64]{2,1,0,3:T(8,128)S(1)}, f32[2,8,16,64]{2,1,0,3:T(8,128)S(1)}, u32[]{:S(2)}, u32[]{:S(2)}) collective-permute-start(f32[2,8,16,64]{2,1,0,3:T(8,128)S(1)} %broadcast_select_fusion.2), channel_id=1, source_target_pairs={{0,8},{1,9},{2,10},{3,11},{4,12},{5,13},{6,14},{7,15},{8,0},{9,1},... | collective-permute-start | bytes 196616 | tf_op jit(solution)/shard_map/ppermute | solution.py:28
  267.5 49.2 %collective-permute-start.6 = (f32[2,8,16,64]{2,1,0,3:T(8,128)S(1)}, f32[2,8,16,64]{2,1,0,3:T(8,128)S(1)}, u32[]{:S(2)}, u32[]{:S(2)}) collective-permute-start(f32[2,8,16,64]{2,1,0,3:T(8,128)S(1)} %broadcast_select_fusion.18), channel_id=1, source_target_pairs={{0,16},{1,17},{2,18},{3,19},{4,20},{5,21},{6,22},{7,23},{8,24},{9,... | collective-permute-start | bytes 196616 | tf_op jit(solution)/shard_map/ppermute | solution.py:28
  296.5 21.4 %collective-permute-start.11 = (f32[2,8,16,64]{2,1,0,3:T(8,128)S(1)}, f32[2,8,16,64]{2,1,0,3:T(8,128)S(1)}, u32[]{:S(2)}, u32[]{:S(2)}) collective-permute-start(f32[2,8,16,64]{2,1,0,3:T(8,128)S(1)} %broadcast_select_fusion.13), channel_id=1, source_target_pairs={{0,16},{1,17},{2,18},{3,19},{4,20},{5,21},{6,22},{7,23},{8,24},{9,... | collective-permute-start | bytes 196616 | tf_op jit(solution)/shard_map/ppermute | solution.py:28
  299.7 17.5 %copy-start.18 = (f32[64,16]{0,1:T(8,128)S(1)}, f32[64,16]{0,1:T(8,128)}, u32[]{:S(2)}) copy-start(f32[64,16]{0,1:T(8,128)} %param.15) | copy-start | bytes 12292
  313.4 16.3 %collective-permute-start.16 = (f32[2,8,16,64]{2,1,0,3:T(8,128)S(1)}, f32[2,8,16,64]{2,1,0,3:T(8,128)S(1)}, u32[]{:S(2)}, u32[]{:S(2)}) collective-permute-start(f32[2,8,16,64]{2,1,0,3:T(8,128)S(1)} %broadcast_select_fusion.8), channel_id=1, source_target_pairs={{0,16},{1,17},{2,18},{3,19},{4,20},{5,21},{6,22},{7,23},{8,24},{9,... | collective-permute-start | bytes 196616 | tf_op jit(solution)/shard_map/ppermute | solution.py:28
  316.7 22.7 %collective-permute-start.21 = (f32[2,8,16,64]{2,1,0,3:T(8,128)S(1)}, f32[2,8,16,64]{2,1,0,3:T(8,128)S(1)}, u32[]{:S(2)}, u32[]{:S(2)}) collective-permute-start(f32[2,8,16,64]{2,1,0,3:T(8,128)S(1)} %broadcast_select_fusion.3), channel_id=1, source_target_pairs={{0,16},{1,17},{2,18},{3,19},{4,20},{5,21},{6,22},{7,23},{8,24},{9,... | collective-permute-start | bytes 196616 | tf_op jit(solution)/shard_map/ppermute | solution.py:28
  (23 other events, 88.3 us)
where the time goes:
time: 373 us; the launch traced here: 372 us
  waiting for transfers between devices  183 us (49%)
  starting transfers between devices  107 us (29%)
  other arithmetic  32.4 us (9%)
  local copies, waits for them, and re-layouts  23.8 us (6%)
  matrix products  12.9 us (3%)
  between operations  12.5 us (3%)
    ppermute x20, waiting for transfers between devices, from_partner(): lax.ppermute(value, axis, [(i, i ^ 1 << bit) for i in range(lax.axis_size...  183 us
    ppermute x20, starting transfers between devices, from_partner(): lax.ppermute(value, axis, [(i, i ^ 1 << bit) for i in range(lax.axis_size...  103 us
    scatter-add x4, other arithmetic, local(): image = image.at[:, :, :, recv_elem[step_round]].add(lifted)  19.7 us
    gather x4, local copies, waits for them, and re-layouts, local(): picked = jnp.take(response, send_elem[step_round], axis=3)  9.65 us
    dot_general x4, matrix products, local(): jnp.einsum('sgb,cjbs->cjgs', select, picked, precision=lax.Precision.HIGH...  9.14 us
  transfers between devices with their start and end apart: 22, of which 11 were waited for; matrix products, arithmetic and copies ran while one was open for 11% of the time, Pallas kernels for 0%

commit v1 on v0

v1 whole, which is shorter than its diff:
```python
import jax
import jax.numpy as jnp
from jax import lax
from jax.experimental import pallas as pl
from jax.experimental.pallas import tpu as pltpu
from jax.sharding import PartitionSpec as P

REACH = 8
ROUNDS = 4
CHUNKS = 4
base_omega = 0.2

F32 = jnp.float32
BF16 = jnp.bfloat16
VMEM = pl.BlockSpec(memory_space=pltpu.VMEM)
SMEM = pl.BlockSpec(memory_space=pltpu.SMEM)


def split(value):
    high = value.astype(BF16)
    low = (value - high.astype(F32)).astype(BF16)
    return high, low


def dot(a, b):
    return lax.dot_general(a, b, (((1,), (0,)), ((), ())), preferred_element_type=F32)


def dot_nt(a, b):
    return lax.dot_general(a, b, (((1,), (1,)), ((), ())), preferred_element_type=F32)


def round_rows(masks):
    first = jnp.int32(0)
    last = jnp.int32(0)
    for r in range(ROUNDS):
        smallest = masks[r] == 1
        largest = masks[r] == 31
        first = jnp.where(smallest, r, first)
        last = jnp.where(largest, r, last)
    mid_a = jnp.int32(0)
    mid_b = jnp.int32(0)
    for r in range(ROUNDS):
        middle = jnp.logical_and(first != r, last != r)
        mid_b = jnp.where(middle, r, mid_b)
        back = ROUNDS - 1 - r
        middle = jnp.logical_and(first != back, last != back)
        mid_a = jnp.where(middle, back, mid_a)
    return first, last, mid_a, mid_b


def slot_row(ref, rows):
    return jnp.concatenate([ref[pl.ds(r, 1), :] for r in rows], axis=1)


def trace_kernel(masks, response, trace_mats, send_elem, send_face, small, large, middle, lane_masks):
    rows = round_rows(masks)
    elems = slot_row(send_elem, rows)
    faces = slot_row(send_face, rows)
    harm_count, unknowns, elements = response.shape[1:]
    slots = elems.shape[1]
    half = slots // 4
    pick = (lax.broadcasted_iota(jnp.int32, (elements, slots), 0) == elems).astype(F32).astype(BF16)
    mats = trace_mats[...].reshape(-1, unknowns)
    m_high, m_low = split(mats)
    stack = jnp.concatenate([m_high, m_low, m_high], axis=1)
    face_vars = mats.shape[0] // 4
    left = lax.broadcasted_iota(jnp.int32, (face_vars, 2 * half), 1) < half

    def traced(c, j):
        high, low = split(response[c, j])
        p_high = dot(high, pick).astype(BF16)
        p_low = dot(low, pick).astype(BF16)
        out = dot(stack, jnp.concatenate([p_high, p_high, p_low], axis=0))
        total = jnp.zeros((face_vars, slots), F32)
        for face_id in range(4):
            total = total + jnp.where(
                faces == face_id, out[face_id * face_vars:(face_id + 1) * face_vars], 0.0
            )
        return total

    for j in range(harm_count):
        real = traced(0, j)
        imag = traced(1, j)
        ends_r, ends_i = real[:, :2 * half], imag[:, :2 * half]
        small[j] = jnp.where(left, ends_r, pltpu.roll(ends_i, half, 1))
        large[j] = jnp.where(left, pltpu.roll(ends_r, half, 1), ends_i)
        middle[0, j] = real[:, 2 * half:]
        middle[1, j] = imag[:, 2 * half:]
    lane = lax.broadcasted_iota(jnp.int32, lane_masks.shape, 1)
    lane_masks[...] = jnp.where(lane < half, masks[rows[2]], masks[rows[3]])


def tiles(unknowns, elements, body):
    cols = elements // 128
    def step(t, carry):
        r = pl.ds(pl.multiple_of((t // cols) * 8, 8), 8)
        e = pl.ds(pl.multiple_of((t % cols) * 128, 128), 128)
        body(r, e)
        return carry
    lax.fori_loop(0, (unknowns // 8) * cols, step, 0)


def conv_pairs(get_in, coeff, r, e, pairs, acc_r, acc_i):
    for i, m in pairs:
        c_r = coeff[0, m, r, e]
        c_i = coeff[1, m, r, e]
        x_r, x_i = get_in(i)
        acc_r = acc_r + c_r * x_r - c_i * x_i
        acc_i = acc_i + c_r * x_i + c_i * x_r
    return acc_r, acc_i


def high_pairs(j, count):
    return [(i, j - i) for i in range(j + 1)]


def low_pairs(j, count):
    return [(i, 2 * REACH + j - i) for i in range(j, count)]


def own_pairs(j, count):
    return [(i, REACH + j - i) for i in range(count)]


def conv_kernel(response, coeff, *refs):
    chunks, acc = refs[:-1], refs[-1]
    harm_count, unknowns, elements = response.shape[1:]
    odd = lax.axis_index("harm") % 2
    width = chunks[0].shape[1]

    def run(side_pairs):
        def body(r, e):
            own = [(response[0, i, r, e], response[1, i, r, e]) for i in range(harm_count)]
            side = [
                (chunks[i // width][0, i % width, r, e], chunks[i // width][1, i % width, r, e])
                for i in range(harm_count)
            ]
            for j in range(harm_count):
                a = jnp.zeros((8, 128), F32)
                a_r, a_i = conv_pairs(lambda i: own[i], coeff, r, e, own_pairs(j, harm_count), a, a)
                a_r, a_i = conv_pairs(lambda i: side[i], coeff, r, e, side_pairs(j, harm_count), a_r, a_i)
                acc[0, j, r, e] = a_r
                acc[1, j, r, e] = a_i
        tiles(unknowns, elements, body)

    @pl.when(odd == 0)
    def _():
        run(high_pairs)

    @pl.when(odd == 1)
    def _():
        run(low_pairs)


def final_kernel(
    masks, response, coeff, acc, volume_mat, lift_mat, recv_elem, small, large, middle, *refs
):
    chunks, out, conv = refs[:-2], refs[-2], refs[-1]
    harm_count, unknowns, elements = response.shape[1:]
    harm = lax.axis_index("harm")
    odd = harm % 2
    width = chunks[0].shape[1]

    def run(side_pairs):
        def body(r, e):
            side = [
                (chunks[i // width][0, i % width, r, e], chunks[i // width][1, i % width, r, e])
                for i in range(harm_count)
            ]
            for j in range(harm_count):
                a_r, a_i = conv_pairs(
                    lambda i: side[i], coeff, r, e, side_pairs(j, harm_count),
                    acc[0, j, r, e], acc[1, j, r, e],
                )
                conv[0, j, r, e] = a_r
                conv[1, j, r, e] = a_i
        tiles(unknowns, elements, body)

    @pl.when(odd == 0)
    def _():
        run(low_pairs)

    @pl.when(odd == 1)
    def _():
        run(high_pairs)

    rows = round_rows(masks)
    elems = slot_row(recv_elem, rows)
    slots = elems.shape[1]
    half = slots // 4
    place = (lax.broadcasted_iota(jnp.int32, (elements, slots), 0) == elems).astype(F32).astype(BF16)
    v_high, v_low = split(volume_mat[...])
    l_high, l_low = split(lift_mat[...])
    stack = jnp.concatenate([v_high, v_low, v_high, l_high, l_low, l_high], axis=1)
    face_vars = lift_mat.shape[1]
    left = lax.broadcasted_iota(jnp.int32, (face_vars, 2 * half), 1) < half
    period = lax.axis_size("harm") * harm_count
    for j in range(harm_count):
        got_s, got_l = small[j], large[j]
        ends_r = jnp.where(left, got_s, pltpu.roll(got_l, half, 1))
        ends_i = jnp.where(left, pltpu.roll(got_s, half, 1), got_l)
        slot = harm * harm_count + j
        wave = jnp.where(slot < period // 2, slot, slot - period).astype(F32)
        frequency = base_omega * wave
        for c, ends in ((0, ends_r), (1, ends_i)):
            got = jnp.concatenate([ends, middle[c, j]], axis=1)
            g_high, g_low = split(got)
            q = dot_nt(g_high, place) + dot_nt(g_low, place)
            q_high, q_low = split(q)
            x_high, x_low = split(conv[c, j])
            image = dot(stack, jnp.concatenate([x_high, x_high, x_low, q_high, q_high, q_low], axis=0))
            if c == 0:
                out[0, j] = image - frequency * response[1, j]
            else:
                out[1, j] = image + frequency * response[0, j]


def from_partner(value, axis, mask):
    return lax.ppermute(value, axis, [(i, i ^ mask) for i in range(lax.axis_size(axis))])


def local(
    response,
    base_coeff,
    volume_mat,
    trace_mats,
    lift_mat,
    round_masks,
    send_elem,
    send_face,
    recv_elem,
):
    harm_count, unknowns, elements = response.shape[1:]
    groups = lax.axis_size("harm")
    parts = lax.axis_size("dom")
    width = harm_count // CHUNKS
    near, far = [], []
    skip = [(i, (i + 2) % groups if i % 2 == 0 else (i - 2) % groups) for i in range(groups)]
    for k in range(CHUNKS):
        piece = response[:, k * width:(k + 1) * width]
        near.append(from_partner(piece, "harm", 1))
    for k in range(CHUNKS):
        far.append(lax.ppermute(near[k], "harm", skip))

    face_vars = trace_mats.shape[1]
    slots = send_elem.shape[1]
    ends_shape = jax.ShapeDtypeStruct((harm_count, face_vars, 2 * slots), F32)
    small, large, middle, lane_masks = pl.pallas_call(
        trace_kernel,
        name="traces",
        in_specs=[SMEM] + [VMEM] * 4,
        out_specs=[VMEM] * 4,
        out_shape=[
            ends_shape,
            ends_shape,
            jax.ShapeDtypeStruct((2, harm_count, face_vars, 2 * slots), F32),
            jax.ShapeDtypeStruct((1, 2 * slots), jnp.int32),
        ],
    )(round_masks, response, trace_mats, send_elem, send_face)
    small = from_partner(small, "dom", 1)
    large = from_partner(large, "dom", parts - 1)
    for bit in (0, 4, 1, 2, 3):
        swapped = from_partner(middle, "dom", 1 << bit)
        chosen = jnp.bitwise_and(jnp.right_shift(lane_masks, bit), 1) == 1
        middle = jnp.where(chosen[:, None, None], swapped, middle)

    acc = pl.pallas_call(
        conv_kernel,
        name="conv_near",
        in_specs=[VMEM] * (2 + CHUNKS),
        out_specs=VMEM,
        out_shape=jax.ShapeDtypeStruct(response.shape, F32),
    )(response, base_coeff, *near)
    return pl.pallas_call(
        final_kernel,
        name="finish",
        in_specs=[SMEM] + [VMEM] * (9 + CHUNKS),
        out_specs=VMEM,
        out_shape=jax.ShapeDtypeStruct(response.shape, F32),
        scratch_shapes=[pltpu.VMEM(response.shape, F32)],
    )(
        round_masks, response, base_coeff, acc, volume_mat, lift_mat, recv_elem,
        small, large, middle, *far,
    )


def solution(mesh):
    in_specs = (
        P(None, "harm", None, "dom"),
        P(None, None, None, "dom"),
        P(),
        P(),
        P(),
        P(),
        P(None, "dom"),
        P(None, "dom"),
        P(None, "dom"),
    )
    out_specs = P(None, "harm", None, "dom")
    return jax.shard_map(local, mesh=mesh, in_specs=in_specs, out_specs=out_specs, check_vma=False)
```

time: 373 us -> 75.8 us (0.20)
  the two profiles are of different devices: /device:TPU:96 before, /device:TPU:1 now
where the time goes in v1:
time: 75.8 us; the launch traced here: 75.7 us
  starting transfers between devices  31.6 us (42%)
  waiting for transfers between devices  19.9 us (26%)
  Pallas kernels  19.5 us (26%)
  local copies, waits for them, and re-layouts  2.37 us (3%)
  other arithmetic  2.27 us (3%)
    ppermute x11, starting transfers between devices, from_partner(): lax.ppermute(value, axis, [(i, i ^ mask) for i in range(lax.axis_size(axi...  26.8 us
    ppermute x11, waiting for transfers between devices, from_partner(): lax.ppermute(value, axis, [(i, i ^ mask) for i in range(lax.axis_size(axi...  19.9 us
    pallas_call x1, Pallas kernels, local(): pl.pallas_call(final_kernel, name='finish', in_specs=[SMEM] + [VMEM] * (9...  9 us
    pallas_call x1, Pallas kernels, local(): pl.pallas_call(conv_kernel, name='conv_near', in_specs=[VMEM] * (2 + CHUN...  5.48 us
    pallas_call x1, Pallas kernels, local(): pl.pallas_call(trace_kernel, name='traces', in_specs=[SMEM] + [VMEM] * 4,...  4.99 us
    ppermute x4, starting transfers between devices, local(): far.append(lax.ppermute(near[k], 'harm', skip))  4.83 us
    unnamed x27, local copies, waits for them, and re-layouts  2.28 us
    select_n x5, other arithmetic, local(): middle = jnp.where(chosen[:, None, None], swapped, middle)  1.64 us
  transfers between devices with their start and end apart: 15, of which 7 were waited for; matrix products, arithmetic and copies ran while one was open for 3% of the time, Pallas kernels for 7%

profile of v1, /device:TPU:1, one launch (start us, length us, event | category | flops | bytes accessed | tf_op | source)
XLA Modules:
  0.0 75.7 jit_solution(1510629899608767547)
XLA Ops:
  0.0 5.0 %traces.1 = (f32[8,16,128]{2,1,0:T(8,128)}, f32[8,16,128]{2,1,0:T(8,128)}, f32[2,8,16,128]{3,2,1,0:T(8,128)}, s32[1,128]{1,0:T(1,128)}) custom-call(s32[4]{0:T(128)} %masks.3, f32[2,8,64,256]{3,2,1,0:T(8,128)} %response.5, f32[4,16,64]{2,1,0:T(8,128)} %trace_mats.1, s32[4,64]{1,0:T(4,128)} %send_elem.1, s32[4,64]{1,0:T(4,128)} %send_face.1), custom_call_target="tpu_custom_call" | custom-call | tf_op jit(solution)/shard_map/traces/pallas_call | solution.py:249
  5.0 3.2 %collective-permute-start.6 = (f32[2,8,16,128]{3,2,1,0:T(8,128)}, f32[2,8,16,128]{3,2,1,0:T(8,128)S(1)}, u32[]{:S(2)}, u32[]{:S(2)}) collective-permute-start(f32[2,8,16,128]{3,2,1,0:T(8,128)} %get-tuple-element.12), channel_id=1, source_target_pairs={{0,1},{1,0},{2,3},{3,2},{4,5},{5,4},{6,7},{7,6},{8,9},{9,8},{10,11... | collective-permute-start | bytes 393224 | tf_op jit(solution)/shard_map/ppermute | solution.py:220
  9.4 0.9 %broadcast_select_fusion = f32[2,8,16,128]{3,2,1,0:T(8,128)S(1)} fusion(f32[2,8,16,128]{3,2,1,0:T(8,128)S(1)} %collective-permute-done.6, f32[2,8,16,128]{3,2,1,0:T(8,128)} %get-tuple-element.12, pred[128]{0:T(512)(128)(4,1)S(1)} %get-tuple-element.18), kind=kLoop, calls=%fused_computation | loop fusion | flops 32768 | bytes 393344 | tf_op jit(solution)/shard_map/jit(_where)/select_n | solution.py:266
  10.3 1.3 %collective-permute-start.7 = (f32[2,8,16,128]{3,2,1,0:T(8,128)S(1)}, f32[2,8,16,128]{3,2,1,0:T(8,128)S(1)}, u32[]{:S(2)}, u32[]{:S(2)}) collective-permute-start(f32[2,8,16,128]{3,2,1,0:T(8,128)S(1)} %broadcast_select_fusion), channel_id=1, source_target_pairs={{0,16},{1,17},{2,18},{3,19},{4,20},{5,21},{6,22},{7,23},{8,24},{9,... | collective-permute-start | bytes 393224 | tf_op jit(solution)/shard_map/ppermute | solution.py:220
  11.6 5.0 %collective-permute-done.7 = f32[2,8,16,128]{3,2,1,0:T(8,128)S(1)} collective-permute-done((f32[2,8,16,128]{3,2,1,0:T(8,128)S(1)}, f32[2,8,16,128]{3,2,1,0:T(8,128)S(1)}, u32[]{:S(2)}, u32[]{:S(2)}) %collective-permute-start.7) | collective-permute-done | bytes 131104 | tf_op jit(solution)/shard_map/ppermute | solution.py:220
  16.7 1.4 %collective-permute-start.4 = (f32[8,16,128]{2,1,0:T(8,128)}, f32[8,16,128]{2,1,0:T(8,128)S(1)}, u32[]{:S(2)}, u32[]{:S(2)}) collective-permute-start(f32[8,16,128]{2,1,0:T(8,128)} %get-tuple-element.9), channel_id=1, source_target_pairs={{0,1},{1,0},{2,3},{3,2},{4,5},{5,4},{6,7},{7,6},{8,9},{9,8},{10,11... | collective-permute-start | bytes 196616 | tf_op jit(solution)/shard_map/ppermute | solution.py:220
  18.1 2.4 %collective-permute-done.8 = f32[2,8,16,128]{3,2,1,0:T(8,128)S(1)} collective-permute-done((f32[2,8,16,128]{3,2,1,0:T(8,128)S(1)}, f32[2,8,16,128]{3,2,1,0:T(8,128)S(1)}, u32[]{:S(2)}, u32[]{:S(2)}) %collective-permute-start.8) | collective-permute-done | bytes 131104 | tf_op jit(solution)/shard_map/ppermute | solution.py:220
  20.5 1.5 %collective-permute-start.9 = (f32[2,8,16,128]{3,2,1,0:T(8,128)S(1)}, f32[2,8,16,128]{3,2,1,0:T(8,128)S(1)}, u32[]{:S(2)}, u32[]{:S(2)}) collective-permute-start(f32[2,8,16,128]{3,2,1,0:T(8,128)S(1)} %broadcast_select_fusion.2), channel_id=1, source_target_pairs={{0,4},{1,5},{2,6},{3,7},{4,0},{5,1},{6,2},{7,3},{8,12},{9,13},{10,... | collective-permute-start | bytes 393224 | tf_op jit(solution)/shard_map/ppermute | solution.py:220
  22.2 1.4 %collective-permute-start.3 = (f32[2,2,64,256]{3,2,1,0:T(8,128)S(1)}, f32[2,2,64,256]{3,2,1,0:T(8,128)S(1)}, u32[]{:S(2)}, u32[]{:S(2)}) collective-permute-start(f32[2,2,64,256]{3,2,1,0:T(8,128)S(1)} %get-tuple-element.13), channel_id=1, source_target_pairs={{0,32},{32,0},{64,96},{96,64},{128,160},{160,128},{192,224},{224,1... | collective-permute-start | bytes 786440 | tf_op jit(solution)/shard_map/ppermute | solution.py:220
  23.8 1.3 %collective-permute-start.1 = (f32[2,2,64,256]{3,2,1,0:T(8,128)S(1)}, f32[2,2,64,256]{3,2,1,0:T(8,128)S(1)}, u32[]{:S(2)}, u32[]{:S(2)}) collective-permute-start(f32[2,2,64,256]{3,2,1,0:T(8,128)S(1)} %get-tuple-element.15), channel_id=1, source_target_pairs={{0,32},{32,0},{64,96},{96,64},{128,160},{160,128},{192,224},{224,1... | collective-permute-start | bytes 786440 | tf_op jit(solution)/shard_map/ppermute | solution.py:220
  25.1 1.7 %collective-permute-done.9 = f32[2,8,16,128]{3,2,1,0:T(8,128)S(1)} collective-permute-done((f32[2,8,16,128]{3,2,1,0:T(8,128)S(1)}, f32[2,8,16,128]{3,2,1,0:T(8,128)S(1)}, u32[]{:S(2)}, u32[]{:S(2)}) %collective-permute-start.9) | collective-permute-done | bytes 131104 | tf_op jit(solution)/shard_map/ppermute | solution.py:220
  26.8 0.8 %collective-permute-start = (f32[2,2,64,256]{3,2,1,0:T(8,128)S(1)}, f32[2,2,64,256]{3,2,1,0:T(8,128)S(1)}, u32[]{:S(2)}, u32[]{:S(2)}) collective-permute-start(f32[2,2,64,256]{3,2,1,0:T(8,128)S(1)} %get-tuple-element.16), channel_id=1, source_target_pairs={{0,32},{32,0},{64,96},{96,64},{128,160},{160,128},{192,224},{224,1... | collective-permute-start | bytes 786440 | tf_op jit(solution)/shard_map/ppermute | solution.py:220
  27.6 5.8 %collective-permute-start.10 = (f32[2,8,16,128]{3,2,1,0:T(8,128)S(1)}, f32[2,8,16,128]{3,2,1,0:T(8,128)S(1)}, u32[]{:S(2)}, u32[]{:S(2)}) collective-permute-start(f32[2,8,16,128]{3,2,1,0:T(8,128)S(1)} %broadcast_select_fusion.3), channel_id=1, source_target_pairs={{0,8},{1,9},{2,10},{3,11},{4,12},{5,13},{6,14},{7,15},{8,0},{9,1},... | collective-permute-start | bytes 393224 | tf_op jit(solution)/shard_map/ppermute | solution.py:220
  33.4 1.2 %collective-permute-start.14 = (f32[2,2,64,256]{3,2,1,0:T(8,128)S(1)}, f32[2,2,64,256]{3,2,1,0:T(8,128)S(1)}, u32[]{:S(2)}, u32[]{:S(2)}) collective-permute-start(f32[2,2,64,256]{3,2,1,0:T(8,128)S(1)} %collective-permute-done.3.refs_3_), channel_id=1, source_target_pairs={{0,64},{32,224},{64,128},{96,32},{128,192},{160,96},{192,0},{224,1... | collective-permute-start | bytes 786440 | tf_op jit(solution)/shard_map/ppermute | solution.py:244
  34.6 1.2 %collective-permute-start.13 = (f32[2,2,64,256]{3,2,1,0:T(8,128)S(1)}, f32[2,2,64,256]{3,2,1,0:T(8,128)S(1)}, u32[]{:S(2)}, u32[]{:S(2)}) collective-permute-start(f32[2,2,64,256]{3,2,1,0:T(8,128)S(1)} %collective-permute-done.2.refs_2_), channel_id=1, source_target_pairs={{0,64},{32,224},{64,128},{96,32},{128,192},{160,96},{192,0},{224,1... | collective-permute-start | bytes 786440 | tf_op jit(solution)/shard_map/ppermute | solution.py:244
  35.8 3.1 %collective-permute-done.1.refs_1_ = f32[2,2,64,256]{3,2,1,0:T(8,128)S(1)} collective-permute-done((f32[2,2,64,256]{3,2,1,0:T(8,128)S(1)}, f32[2,2,64,256]{3,2,1,0:T(8,128)S(1)}, u32[]{:S(2)}, u32[]{:S(2)}) %collective-permute-start.1) | collective-permute-done | bytes 262176 | tf_op jit(solution)/shard_map/ppermute | solution.py:220
  38.9 1.2 %collective-permute-start.12 = (f32[2,2,64,256]{3,2,1,0:T(8,128)S(1)}, f32[2,2,64,256]{3,2,1,0:T(8,128)S(1)}, u32[]{:S(2)}, u32[]{:S(2)}) collective-permute-start(f32[2,2,64,256]{3,2,1,0:T(8,128)S(1)} %collective-permute-done.1.refs_1_), channel_id=1, source_target_pairs={{0,64},{32,224},{64,128},{96,32},{128,192},{160,96},{192,0},{224,1... | collective-permute-start | bytes 786440 | tf_op jit(solution)/shard_map/ppermute | solution.py:244
  40.1 4.4 %collective-permute-done.refs_0_ = f32[2,2,64,256]{3,2,1,0:T(8,128)S(1)} collective-permute-done((f32[2,2,64,256]{3,2,1,0:T(8,128)S(1)}, f32[2,2,64,256]{3,2,1,0:T(8,128)S(1)}, u32[]{:S(2)}, u32[]{:S(2)}) %collective-permute-start) | collective-permute-done | bytes 262176 | tf_op jit(solution)/shard_map/ppermute | solution.py:220
  44.5 1.2 %collective-permute-start.11 = (f32[2,2,64,256]{3,2,1,0:T(8,128)S(1)}, f32[2,2,64,256]{3,2,1,0:T(8,128)S(1)}, u32[]{:S(2)}, u32[]{:S(2)}) collective-permute-start(f32[2,2,64,256]{3,2,1,0:T(8,128)S(1)} %collective-permute-done.refs_0_), channel_id=1, source_target_pairs={{0,64},{32,224},{64,128},{96,32},{128,192},{160,96},{192,0},{224,1... | collective-permute-start | bytes 786440 | tf_op jit(solution)/shard_map/ppermute | solution.py:244
  46.5 5.5 %conv_near.1.acc = f32[2,8,64,256]{3,2,1,0:T(8,128)} custom-call(f32[2,8,64,256]{3,2,1,0:T(8,128)} %response.5, f32[2,17,64,256]{3,2,1,0:T(8,128)} %coeff.3, f32[2,2,64,256]{3,2,1,0:T(8,128)} %copy-done.8, f32[2,2,64,256]{3,2,1,0:T(8,128)} %copy-done.7, f32[2,2,64,256]{3,2,1,0:T(8,128)} %copy-done.6, f32[2,2,64,256]{3,2,1,0:T(8,128)} %copy-done.5), custom_call_target="tpu_custom_call" | custom-call | tf_op jit(solution)/shard_map/conv_near/pallas_call | solution.py:268
  51.9 9.8 %collective-permute-start.5 = (f32[8,16,128]{2,1,0:T(8,128)S(1)}, f32[8,16,128]{2,1,0:T(8,128)S(1)}, u32[]{:S(2)}, u32[]{:S(2)}) collective-permute-start(f32[8,16,128]{2,1,0:T(8,128)S(1)} %copy-done.12), channel_id=1, source_target_pairs={{0,31},{1,30},{2,29},{3,28},{4,27},{5,26},{6,25},{7,24},{8,23},{9,... | collective-permute-start | bytes 196616 | tf_op jit(solution)/shard_map/ppermute | solution.py:220
  62.4 2.7 %collective-permute-done.5.large = f32[8,16,128]{2,1,0:T(8,128)S(1)} collective-permute-done((f32[8,16,128]{2,1,0:T(8,128)S(1)}, f32[8,16,128]{2,1,0:T(8,128)S(1)}, u32[]{:S(2)}, u32[]{:S(2)}) %collective-permute-start.5) | collective-permute-done | bytes 65568 | tf_op jit(solution)/shard_map/ppermute | solution.py:220
  66.0 0.7 copy-done.4
  66.7 9.0 %finish.1 = f32[2,8,64,256]{3,2,1,0:T(8,128)} custom-call(s32[4]{0:T(128)} %masks.3, f32[2,8,64,256]{3,2,1,0:T(8,128)} %response.5, f32[2,17,64,256]{3,2,1,0:T(8,128)} %coeff.3, f32[2,8,64,256]{3,2,1,0:T(8,128)} %conv_near.1.acc, f32[64,64]{1,0:T(8,128)} %volume_mat.1, f32[64,16]{1,0:T(8,128)} %copy.10.lift_mat, s32[4,64]{1,0:T(4,128)} %recv_elem.1, ...), custom_call_target="tpu_custom_call" | custom-call | tf_op jit(solution)/shard_map/finish/pallas_call | solution.py:275
  (43 shorter events, 3.9 us)
Async XLA Ops:
  0.0 22.1 %copy-start = (f32[2,8,64,256]{3,2,1,0:T(8,128)S(1)}, f32[2,8,64,256]{3,2,1,0:T(8,128)}, u32[]{:S(2)}) copy-start(f32[2,8,64,256]{3,2,1,0:T(8,128)} %response.5) | copy-start | bytes 3145732
  0.0 45.7 %copy-start.11 = (f32[64,16]{0,1:T(8,128)S(1)}, f32[64,16]{0,1:T(8,128)}, u32[]{:S(2)}) copy-start(f32[64,16]{0,1:T(8,128)} %param.13) | copy-start | bytes 12292
  5.0 4.4 %collective-permute-start.6 = (f32[2,8,16,128]{3,2,1,0:T(8,128)}, f32[2,8,16,128]{3,2,1,0:T(8,128)S(1)}, u32[]{:S(2)}, u32[]{:S(2)}) collective-permute-start(f32[2,8,16,128]{3,2,1,0:T(8,128)} %get-tuple-element.12), channel_id=1, source_target_pairs={{0,1},{1,0},{2,3},{3,2},{4,5},{5,4},{6,7},{7,6},{8,9},{9,8},{10,11... | collective-permute-start | bytes 393224 | tf_op jit(solution)/shard_map/ppermute | solution.py:220
  10.3 6.3 %collective-permute-start.7 = (f32[2,8,16,128]{3,2,1,0:T(8,128)S(1)}, f32[2,8,16,128]{3,2,1,0:T(8,128)S(1)}, u32[]{:S(2)}, u32[]{:S(2)}) collective-permute-start(f32[2,8,16,128]{3,2,1,0:T(8,128)S(1)} %broadcast_select_fusion), channel_id=1, source_target_pairs={{0,16},{1,17},{2,18},{3,19},{4,20},{5,21},{6,22},{7,23},{8,24},{9,... | collective-permute-start | bytes 393224 | tf_op jit(solution)/shard_map/ppermute | solution.py:220
  16.6 3.9 %collective-permute-start.8 = (f32[2,8,16,128]{3,2,1,0:T(8,128)S(1)}, f32[2,8,16,128]{3,2,1,0:T(8,128)S(1)}, u32[]{:S(2)}, u32[]{:S(2)}) collective-permute-start(f32[2,8,16,128]{3,2,1,0:T(8,128)S(1)} %broadcast_select_fusion.1), channel_id=1, source_target_pairs={{0,2},{1,3},{2,0},{3,1},{4,6},{5,7},{6,4},{7,5},{8,10},{9,11},{10,... | collective-permute-start | bytes 393224 | tf_op jit(solution)/shard_map/ppermute | solution.py:220
  16.7 10.9 %collective-permute-start.4 = (f32[8,16,128]{2,1,0:T(8,128)}, f32[8,16,128]{2,1,0:T(8,128)S(1)}, u32[]{:S(2)}, u32[]{:S(2)}) collective-permute-start(f32[8,16,128]{2,1,0:T(8,128)} %get-tuple-element.9), channel_id=1, source_target_pairs={{0,1},{1,0},{2,3},{3,2},{4,5},{5,4},{6,7},{7,6},{8,9},{9,8},{10,11... | collective-permute-start | bytes 196616 | tf_op jit(solution)/shard_map/ppermute | solution.py:220
  20.5 6.2 %collective-permute-start.9 = (f32[2,8,16,128]{3,2,1,0:T(8,128)S(1)}, f32[2,8,16,128]{3,2,1,0:T(8,128)S(1)}, u32[]{:S(2)}, u32[]{:S(2)}) collective-permute-start(f32[2,8,16,128]{3,2,1,0:T(8,128)S(1)} %broadcast_select_fusion.2), channel_id=1, source_target_pairs={{0,4},{1,5},{2,6},{3,7},{4,0},{5,1},{6,2},{7,3},{8,12},{9,13},{10,... | collective-permute-start | bytes 393224 | tf_op jit(solution)/shard_map/ppermute | solution.py:220
  22.2 11.2 %collective-permute-start.3 = (f32[2,2,64,256]{3,2,1,0:T(8,128)S(1)}, f32[2,2,64,256]{3,2,1,0:T(8,128)S(1)}, u32[]{:S(2)}, u32[]{:S(2)}) collective-permute-start(f32[2,2,64,256]{3,2,1,0:T(8,128)S(1)} %get-tuple-element.13), channel_id=1, source_target_pairs={{0,32},{32,0},{64,96},{96,64},{128,160},{160,128},{192,224},{224,1... | collective-permute-start | bytes 786440 | tf_op jit(solution)/shard_map/ppermute | solution.py:220
  23.6 11.0 %collective-permute-start.2 = (f32[2,2,64,256]{3,2,1,0:T(8,128)S(1)}, f32[2,2,64,256]{3,2,1,0:T(8,128)S(1)}, u32[]{:S(2)}, u32[]{:S(2)}) collective-permute-start(f32[2,2,64,256]{3,2,1,0:T(8,128)S(1)} %get-tuple-element.14), channel_id=1, source_target_pairs={{0,32},{32,0},{64,96},{96,64},{128,160},{160,128},{192,224},{224,1... | collective-permute-start | bytes 786440 | tf_op jit(solution)/shard_map/ppermute | solution.py:220
  23.8 15.2 %collective-permute-start.1 = (f32[2,2,64,256]{3,2,1,0:T(8,128)S(1)}, f32[2,2,64,256]{3,2,1,0:T(8,128)S(1)}, u32[]{:S(2)}, u32[]{:S(2)}) collective-permute-start(f32[2,2,64,256]{3,2,1,0:T(8,128)S(1)} %get-tuple-element.15), channel_id=1, source_target_pairs={{0,32},{32,0},{64,96},{96,64},{128,160},{160,128},{192,224},{224,1... | collective-permute-start | bytes 786440 | tf_op jit(solution)/shard_map/ppermute | solution.py:220
  26.8 17.8 %collective-permute-start = (f32[2,2,64,256]{3,2,1,0:T(8,128)S(1)}, f32[2,2,64,256]{3,2,1,0:T(8,128)S(1)}, u32[]{:S(2)}, u32[]{:S(2)}) collective-permute-start(f32[2,2,64,256]{3,2,1,0:T(8,128)S(1)} %get-tuple-element.16), channel_id=1, source_target_pairs={{0,32},{32,0},{64,96},{96,64},{128,160},{160,128},{192,224},{224,1... | collective-permute-start | bytes 786440 | tf_op jit(solution)/shard_map/ppermute | solution.py:220
  27.6 37.5 %copy-start.9 = (f32[8,16,128]{2,1,0:T(8,128)}, f32[8,16,128]{2,1,0:T(8,128)S(1)}, u32[]{:S(2)}) copy-start(f32[8,16,128]{2,1,0:T(8,128)S(1)} %collective-permute-done.4.small) | copy-start | bytes 196612
  27.6 24.3 %collective-permute-start.10 = (f32[2,8,16,128]{3,2,1,0:T(8,128)S(1)}, f32[2,8,16,128]{3,2,1,0:T(8,128)S(1)}, u32[]{:S(2)}, u32[]{:S(2)}) collective-permute-start(f32[2,8,16,128]{3,2,1,0:T(8,128)S(1)} %broadcast_select_fusion.3), channel_id=1, source_target_pairs={{0,8},{1,9},{2,10},{3,11},{4,12},{5,13},{6,14},{7,15},{8,0},{9,1},... | collective-permute-start | bytes 393224 | tf_op jit(solution)/shard_map/ppermute | solution.py:220
  33.4 13.1 %copy-start.5 = (f32[2,2,64,256]{3,2,1,0:T(8,128)}, f32[2,2,64,256]{3,2,1,0:T(8,128)S(1)}, u32[]{:S(2)}) copy-start(f32[2,2,64,256]{3,2,1,0:T(8,128)S(1)} %collective-permute-done.3.refs_3_) | copy-start | bytes 786436
  33.4 31.7 %collective-permute-start.14 = (f32[2,2,64,256]{3,2,1,0:T(8,128)S(1)}, f32[2,2,64,256]{3,2,1,0:T(8,128)S(1)}, u32[]{:S(2)}, u32[]{:S(2)}) collective-permute-start(f32[2,2,64,256]{3,2,1,0:T(8,128)S(1)} %collective-permute-done.3.refs_3_), channel_id=1, source_target_pairs={{0,64},{32,224},{64,128},{96,32},{128,192},{160,96},{192,0},{224,1... | collective-permute-start | bytes 786440 | tf_op jit(solution)/shard_map/ppermute | solution.py:244
  34.6 11.8 %copy-start.6 = (f32[2,2,64,256]{3,2,1,0:T(8,128)}, f32[2,2,64,256]{3,2,1,0:T(8,128)S(1)}, u32[]{:S(2)}) copy-start(f32[2,2,64,256]{3,2,1,0:T(8,128)S(1)} %collective-permute-done.2.refs_2_) | copy-start | bytes 786436
  34.6 30.5 %collective-permute-start.13 = (f32[2,2,64,256]{3,2,1,0:T(8,128)S(1)}, f32[2,2,64,256]{3,2,1,0:T(8,128)S(1)}, u32[]{:S(2)}, u32[]{:S(2)}) collective-permute-start(f32[2,2,64,256]{3,2,1,0:T(8,128)S(1)} %collective-permute-done.2.refs_2_), channel_id=1, source_target_pairs={{0,64},{32,224},{64,128},{96,32},{128,192},{160,96},{192,0},{224,1... | collective-permute-start | bytes 786440 | tf_op jit(solution)/shard_map/ppermute | solution.py:244
  38.9 7.5 %copy-start.7 = (f32[2,2,64,256]{3,2,1,0:T(8,128)}, f32[2,2,64,256]{3,2,1,0:T(8,128)S(1)}, u32[]{:S(2)}) copy-start(f32[2,2,64,256]{3,2,1,0:T(8,128)S(1)} %collective-permute-done.1.refs_1_) | copy-start | bytes 786436
  38.9 26.2 %collective-permute-start.12 = (f32[2,2,64,256]{3,2,1,0:T(8,128)S(1)}, f32[2,2,64,256]{3,2,1,0:T(8,128)S(1)}, u32[]{:S(2)}, u32[]{:S(2)}) collective-permute-start(f32[2,2,64,256]{3,2,1,0:T(8,128)S(1)} %collective-permute-done.1.refs_1_), channel_id=1, source_target_pairs={{0,64},{32,224},{64,128},{96,32},{128,192},{160,96},{192,0},{224,1... | collective-permute-start | bytes 786440 | tf_op jit(solution)/shard_map/ppermute | solution.py:244
  44.5 1.9 %copy-start.8 = (f32[2,2,64,256]{3,2,1,0:T(8,128)}, f32[2,2,64,256]{3,2,1,0:T(8,128)S(1)}, u32[]{:S(2)}) copy-start(f32[2,2,64,256]{3,2,1,0:T(8,128)S(1)} %collective-permute-done.refs_0_) | copy-start | bytes 786436
  44.5 20.6 %collective-permute-start.11 = (f32[2,2,64,256]{3,2,1,0:T(8,128)S(1)}, f32[2,2,64,256]{3,2,1,0:T(8,128)S(1)}, u32[]{:S(2)}, u32[]{:S(2)}) collective-permute-start(f32[2,2,64,256]{3,2,1,0:T(8,128)S(1)} %collective-permute-done.refs_0_), channel_id=1, source_target_pairs={{0,64},{32,224},{64,128},{96,32},{128,192},{160,96},{192,0},{224,1... | collective-permute-start | bytes 786440 | tf_op jit(solution)/shard_map/ppermute | solution.py:244
  46.5 5.5 %copy-start.12 = (f32[8,16,128]{2,1,0:T(8,128)S(1)}, f32[8,16,128]{2,1,0:T(8,128)}, u32[]{:S(2)}) copy-start(f32[8,16,128]{2,1,0:T(8,128)} %get-tuple-element.10) | copy-start | bytes 196612
  51.9 13.1 %collective-permute-start.5 = (f32[8,16,128]{2,1,0:T(8,128)S(1)}, f32[8,16,128]{2,1,0:T(8,128)S(1)}, u32[]{:S(2)}, u32[]{:S(2)}) collective-permute-start(f32[8,16,128]{2,1,0:T(8,128)S(1)} %copy-done.12), channel_id=1, source_target_pairs={{0,31},{1,30},{2,29},{3,28},{4,27},{5,26},{6,25},{7,24},{8,23},{9,... | collective-permute-start | bytes 196616 | tf_op jit(solution)/shard_map/ppermute | solution.py:220
  65.1 0.9 %copy-start.3 = (f32[2,2,64,256]{3,2,1,0:T(8,128)}, f32[2,2,64,256]{3,2,1,0:T(8,128)S(1)}, u32[]{:S(2)}) copy-start(f32[2,2,64,256]{3,2,1,0:T(8,128)S(1)} %collective-permute-done.12.refs_1_) | copy-start | bytes 786436
  (4 other events, 2.9 us)

commit v2 on v1

v2 whole, which is shorter than its diff:
```python
import jax
import jax.numpy as jnp
from jax import lax
from jax.experimental import pallas as pl
from jax.experimental.pallas import tpu as pltpu
from jax.sharding import PartitionSpec as P


REACH = 8
ROUNDS = 4
WIDTHS = (2, 2, 2, 1, 1)
EARLY = 2
base_omega = 0.2

F32 = jnp.float32
BF16 = jnp.bfloat16
KERNEL_MEMORY = pltpu.CompilerParams(vmem_limit_bytes=8 * 2**20)
HBM = pl.BlockSpec(memory_space=pl.ANY)
VMEM = pl.BlockSpec(memory_space=pltpu.VMEM)
SMEM = pl.BlockSpec(memory_space=pltpu.SMEM)


def split(value):
    high = value.astype(BF16)
    low = (value - high.astype(F32)).astype(BF16)
    return high, low


def dot(a, b):
    return lax.dot_general(a, b, (((1,), (0,)), ((), ())), preferred_element_type=F32)


def dot_nt(a, b):
    return lax.dot_general(a, b, (((1,), (1,)), ((), ())), preferred_element_type=F32)


def round_rows(masks):
    first = jnp.int32(0)
    last = jnp.int32(0)
    for r in range(ROUNDS):
        smallest = masks[r] == 1
        largest = masks[r] == 31
        first = jnp.where(smallest, r, first)
        last = jnp.where(largest, r, last)
    mid_a = jnp.int32(0)
    mid_b = jnp.int32(0)
    for r in range(ROUNDS):
        middle = jnp.logical_and(first != r, last != r)
        mid_b = jnp.where(middle, r, mid_b)
        back = ROUNDS - 1 - r
        middle = jnp.logical_and(first != back, last != back)
        mid_a = jnp.where(middle, back, mid_a)
    return first, last, mid_a, mid_b


def slot_row(ref, rows):
    return jnp.concatenate([ref[pl.ds(r, 1), :] for r in rows], axis=1)


def cut_kernel(response, whole, *refs):
    pieces, sems = refs[:-1], refs[-1]
    odd = lax.axis_index("harm") % 2
    count = response.shape[1]
    copies = []
    for k, piece in enumerate(pieces):
        first = jnp.where(
            odd == 1, chunk_harmonics(k, count, False)[0], chunk_harmonics(k, count, True)[0]
        )
        copies.append(
            pltpu.make_async_copy(response.at[:, pl.ds(first, WIDTHS[k])], piece, sems.at[k])
        )
    copies.append(pltpu.make_async_copy(response, whole, sems.at[len(pieces)]))
    for copy in copies:
        copy.start()
    for copy in copies:
        copy.wait()


def trace_kernel(masks, response, trace_mats, send_elem, send_face, staged, stay_put, large, lane_bits, p_high, p_low):
    rows = round_rows(masks)
    elems = slot_row(send_elem, rows)
    faces = slot_row(send_face, rows)
    harm_count, unknowns, elements = response.shape[1:]
    slots = elems.shape[1]
    half = slots // 4
    pick = (lax.broadcasted_iota(jnp.int32, (elements, slots), 0) == elems).astype(F32).astype(BF16)
    high, low = split(response[...].reshape(-1, elements))
    p_high[...] = dot(high, pick).astype(BF16)
    p_low[...] = dot(low, pick).astype(BF16)
    mats = trace_mats[...].reshape(-1, unknowns)
    m_high, m_low = split(mats)
    stack = jnp.concatenate([m_high, m_low, m_high], axis=1)
    face_vars = mats.shape[0] // 4
    left = lax.broadcasted_iota(jnp.int32, (face_vars, 2 * half), 1) < half

    def traced(c, j):
        at = pl.ds((c * harm_count + j) * unknowns, unknowns)
        top = p_high[at, :]
        out = dot(stack, jnp.concatenate([top, top, p_low[at, :]], axis=0))
        total = jnp.zeros((face_vars, slots), F32)
        for face_id in range(4):
            total = total + jnp.where(
                faces == face_id, out[face_id * face_vars:(face_id + 1) * face_vars], 0.0
            )
        return total

    for j in range(harm_count):
        real = traced(0, j)
        imag = traced(1, j)
        ends_r, ends_i = real[:, :2 * half], imag[:, :2 * half]
        staged[2 * harm_count + j] = jnp.where(left, ends_r, pltpu.roll(ends_i, half, 1))
        large[j] = jnp.where(left, pltpu.roll(ends_r, half, 1), ends_i)
        for row, value in ((j, real), (harm_count + j, imag)):
            staged[row] = value[:, 2 * half:]
            stay_put[row] = value[:, 2 * half:]
    lane = lax.broadcasted_iota(jnp.int32, (1, 2 * half), 1)
    mask = jnp.where(lane < half, masks[rows[2]], masks[rows[3]])
    bits = [jnp.bitwise_and(jnp.right_shift(mask, b), 1) for b in range(5)]
    for row, bit in enumerate((bits[0], bits[1], jnp.bitwise_xor(bits[2], bits[3]), bits[3], bits[4])):
        lane_bits[row:row + 1, :] = bit


def tiles(unknowns, elements, body):
    cols = elements // 128

    def step(t, carry):
        r = pl.ds(pl.multiple_of((t // cols) * 8, 8), 8)
        e = pl.ds(pl.multiple_of((t % cols) * 128, 128), 128)
        body(r, e)
        return carry

    lax.fori_loop(0, (unknowns // 8) * cols, step, 0)


def add_pair(coeff, m, r, e, x, total):
    c_r = coeff[0, m, r, e]
    c_i = coeff[1, m, r, e]
    add_r = c_r * x[0] - c_i * x[1]
    add_i = c_r * x[1] + c_i * x[0]
    if total is None:
        return add_r, add_i
    return total[0] + add_r, total[1] + add_i


def above(i, j):
    return j - i if i <= j else None


def below(i, j):
    return 2 * REACH + j - i if i >= j else None


def inside(i, j):
    return REACH + j - i


def chunk_harmonics(k, count, ascending):
    done = sum(WIDTHS[:k])
    first = done if ascending else count - done - WIDTHS[k]
    return [first + q for q in range(WIDTHS[k])]


def gather_sources(chunks, first, count, ascending, index):
    return [
        (chunk, q, i, index)
        for k, chunk in enumerate(chunks)
        for q, i in enumerate(chunk_harmonics(first + k, count, ascending))
    ]


def convolve(coeff, sources, r, e, start, outputs):
    values = {}
    for j in outputs:
        total = start(j)
        for n, (ref, at, i, index) in enumerate(sources):
            m = index(i, j)
            if m is None:
                continue
            if n not in values:
                values[n] = (ref[0, at, r, e], ref[1, at, r, e])
            total = add_pair(coeff, m, r, e, values[n], total)
        yield j, total


def by_parity(run):
    odd = lax.axis_index("harm") % 2

    @pl.when(odd == 0)
    def _():
        run(False, above, below)

    @pl.when(odd == 1)
    def _():
        run(True, below, above)


def own_kernel(response, coeff, acc):
    harm_count, unknowns, elements = response.shape[1:]
    sources = [(response, i, i, inside) for i in range(harm_count)]

    def body(r, e):
        for j, total in convolve(coeff, sources, r, e, lambda j: None, range(harm_count)):
            acc[0, j, r, e], acc[1, j, r, e] = total

    tiles(unknowns, elements, body)


def near_kernel(first, coeff, acc, *refs):
    chunks, out = refs[:-1], refs[-1]
    harm_count, unknowns, elements = acc.shape[1:]

    def run(ascending, near_index, far_index):
        sources = gather_sources(chunks, first, harm_count, ascending, near_index)

        def body(r, e):
            start = lambda j: (acc[0, j, r, e], acc[1, j, r, e])
            for j, total in convolve(coeff, sources, r, e, start, range(harm_count)):
                out[0, j, r, e], out[1, j, r, e] = total

        tiles(unknowns, elements, body)

    by_parity(run)


def stacked(mat):
    high, low = split(mat)
    return jnp.concatenate([high, low, high], axis=1)


def product(stack, value):
    high, low = split(value)
    return dot(stack, jnp.concatenate([high, high, low], axis=0))


def main_kernel(coeff, acc, volume_mat, *refs):
    chunks, out, conv = refs[:-2], refs[-2], refs[-1]
    harm_count, unknowns, elements = acc.shape[1:]

    def run(ascending, near_index, far_index):
        sources = gather_sources(chunks, 0, harm_count, ascending, far_index)

        def body(r, e):
            start = lambda j: (acc[0, j, r, e], acc[1, j, r, e])
            for j, total in convolve(coeff, sources, r, e, start, range(harm_count)):
                conv[0, j, r, e], conv[1, j, r, e] = total

        tiles(unknowns, elements, body)

    by_parity(run)
    stack = stacked(volume_mat[...])
    for j in range(harm_count):
        for c in range(2):
            out[c, j] = product(stack, conv[c, j])


def lift_kernel(masks, response, image, lift_mat, recv_elem, small, large, middle, out, edge, got):
    harm_count, _, elements = response.shape[1:]
    harm = lax.axis_index("harm")
    rows = round_rows(masks)
    elems = slot_row(recv_elem, rows)
    slots = elems.shape[1]
    half = slots // 4
    place = (lax.broadcasted_iota(jnp.int32, (elements, slots), 0) == elems).astype(F32).astype(BF16)
    face_vars = lift_mat.shape[1]
    left = lax.broadcasted_iota(jnp.int32, (face_vars, 2 * half), 1) < half
    for j in range(harm_count):
        got_s, got_l = small[2 * harm_count + j], large[j]
        for c in range(2):
            at = pl.ds((c * harm_count + j) * face_vars, face_vars)
            if c == 0:
                got[at, :2 * half] = jnp.where(left, got_s, pltpu.roll(got_l, half, 1))
            else:
                got[at, :2 * half] = jnp.where(left, pltpu.roll(got_s, half, 1), got_l)
            got[at, 2 * half:] = middle[c * harm_count + j]
    g_high, g_low = split(got[...])
    placed = dot_nt(g_high, place) + dot_nt(g_low, place)
    got[...] = placed
    stack = stacked(lift_mat[...])
    period = lax.axis_size("harm") * harm_count
    for j in range(harm_count):
        slot = harm * harm_count + j
        wave = jnp.where(slot < period // 2, slot, slot - period).astype(F32)
        frequency = base_omega * wave
        for c in range(2):
            at = pl.ds((c * harm_count + j) * face_vars, face_vars)
            value = image[c, j] + product(stack, got[at, :])
            if c == 0:
                out[0, j] = value - frequency * response[1, j]
            else:
                out[1, j] = value + frequency * response[0, j]
    width = WIDTHS[-1]
    odd = harm % 2
    edge[...] = out[:, pl.ds(odd * (harm_count - width), width)]


def tail_kernel(coeff, volume_mat, edge, chunk, image, out, conv, sem):
    del image
    width, unknowns, elements = edge.shape[1:]
    harm_count = out.shape[1]
    last = len(WIDTHS) - 1

    def run(ascending, near_index, far_index):
        sources = gather_sources([chunk], last, harm_count, ascending, far_index)
        first = harm_count - width if ascending else 0
        outputs = range(first, first + width)

        def body(r, e):
            for j, total in convolve(coeff, sources, r, e, lambda j: None, outputs):
                conv[0, j - first, r, e], conv[1, j - first, r, e] = total

        tiles(unknowns, elements, body)

    by_parity(run)
    stack = stacked(volume_mat[...])
    for q in range(width):
        for c in range(2):
            conv[c, q] = edge[c, q] + product(stack, conv[c, q])
    odd = lax.axis_index("harm") % 2
    copy = pltpu.make_async_copy(conv, out.at[:, pl.ds(odd * (harm_count - width), width)], sem)
    copy.start()
    copy.wait()


def resident(*values):
    return [pltpu.with_memory_space_constraint(value, pltpu.VMEM) for value in values]


def stay(*values):
    return [pltpu.with_memory_space_constraint(value, pltpu.HBM) for value in values]


def resident_shape(shape, dtype=F32):
    return pltpu.VMEM(shape, dtype)


def from_partner(value, axis, mask):
    return lax.ppermute(value, axis, [(i, i ^ mask) for i in range(lax.axis_size(axis))])


def shape_like(value):
    return jax.ShapeDtypeStruct(value.shape, value.dtype)


def local(
    response,
    base_coeff,
    volume_mat,
    trace_mats,
    lift_mat,
    round_masks,
    send_elem,
    send_face,
    recv_elem,
):
    harm_count, unknowns, elements = response.shape[1:]
    groups = lax.axis_size("harm")
    parts = lax.axis_size("dom")
    skip = [(i, (i + 2) % groups if i % 2 == 0 else (i - 2) % groups) for i in range(groups)]
    near, far = [], []
    whole = response
    response, *pieces = pl.pallas_call(
        cut_kernel,
        name="cut",
        compiler_params=KERNEL_MEMORY,
        in_specs=[HBM],
        out_specs=[VMEM] * (1 + len(WIDTHS)),
        out_shape=[resident_shape(response.shape)]
        + [resident_shape((2, width, unknowns, elements)) for width in WIDTHS],
        scratch_shapes=[pltpu.SemaphoreType.DMA((1 + len(WIDTHS),))],
    )(*stay(response))
    (response,) = resident(response)
    for piece in pieces:
        near.append(from_partner(piece, "harm", 1))
    for k in range(len(WIDTHS)):
        far.append(lax.ppermute(near[k], "harm", skip))

    face_vars = trace_mats.shape[1]
    slots = send_elem.shape[1]
    staged, own, large, lane_bits = pl.pallas_call(
        trace_kernel,
        name="traces",
        compiler_params=KERNEL_MEMORY,
        in_specs=[SMEM] + [VMEM] * 4,
        out_specs=[VMEM] * 4,
        out_shape=[
            resident_shape((3 * harm_count, face_vars, 2 * slots), F32),
            resident_shape((2 * harm_count, face_vars, 2 * slots), F32),
            resident_shape((harm_count, face_vars, 2 * slots), F32),
            resident_shape((8, 2 * slots), jnp.int32),
        ],
        scratch_shapes=[pltpu.VMEM((2 * harm_count * unknowns, 4 * slots), BF16)] * 2,
    )(*stay(round_masks), response, *stay(trace_mats, send_elem, send_face))
    large = from_partner(large, "dom", parts - 1)
    bit = lambda row: lane_bits[row] == 1
    small = from_partner(staged, "dom", 1)
    by_two = from_partner(own, "dom", 2)
    by_three = from_partner(own, "dom", 3)
    middle = jnp.where(
        bit(0), jnp.where(bit(1), by_three, small[:2 * harm_count]), jnp.where(bit(1), by_two, own)
    )
    for stage, mask in enumerate((4, 12, 16), 1):
        swapped = from_partner(middle, "dom", mask)
        middle = jnp.where(bit(stage + 1), swapped, middle)

    acc = pl.pallas_call(
        own_kernel,
        name="own",
        compiler_params=KERNEL_MEMORY,
        in_specs=[VMEM] * 2,
        out_specs=VMEM,
        out_shape=resident_shape(response.shape),
    )(response, *resident(base_coeff))

    def near_call(acc, first, chunks):
        return pl.pallas_call(
            lambda *refs: near_kernel(first, *refs),
            name="near",
            compiler_params=KERNEL_MEMORY,
            in_specs=[VMEM] * (2 + len(chunks)),
            out_specs=VMEM,
            out_shape=resident_shape(response.shape),
        )(*resident(base_coeff, acc, *chunks))

    acc = near_call(acc, 0, near[:EARLY])
    acc = near_call(acc, EARLY, near[EARLY:])
    image = pl.pallas_call(
        main_kernel,
        name="main",
        compiler_params=KERNEL_MEMORY,
        in_specs=[VMEM] * (2 + len(WIDTHS)),
        out_specs=VMEM,
        out_shape=resident_shape(response.shape),
        scratch_shapes=[pltpu.VMEM(response.shape, F32)],
    )(*resident(base_coeff, acc), volume_mat, *resident(*far[:-1]))
    width = WIDTHS[-1]
    edge_shape = (2, width, unknowns, elements)
    image, edge = pl.pallas_call(
        lift_kernel,
        name="lift",
        compiler_params=KERNEL_MEMORY,
        in_specs=[SMEM] + [VMEM] * 7,
        out_specs=[VMEM] * 2,
        out_shape=[shape_like(whole), resident_shape(edge_shape, F32)],
        scratch_shapes=[pltpu.VMEM((2 * harm_count * face_vars, elements), F32)],
    )(*stay(round_masks), response, *resident(image), *stay(lift_mat, recv_elem), *resident(small, large, middle))
    return pl.pallas_call(
        tail_kernel,
        name="tail",
        compiler_params=KERNEL_MEMORY,
        in_specs=[VMEM] * 4 + [HBM],
        out_specs=HBM,
        out_shape=shape_like(whole),
        input_output_aliases={4: 0},
        scratch_shapes=[pltpu.VMEM(edge_shape, F32), pltpu.SemaphoreType.DMA],
    )(*resident(base_coeff), volume_mat, *resident(edge, far[-1]), image)


def solution(mesh):
    in_specs = (
        P(None, "harm", None, "dom"),
        P(None, None, None, "dom"),
        P(),
        P(),
        P(),
        P(),
        P(None, "dom"),
        P(None, "dom"),
        P(None, "dom"),
    )
    out_specs = P(None, "harm", None, "dom")

    return jax.shard_map(local, mesh=mesh, in_specs=in_specs, out_specs=out_specs, check_vma=False)
```

time: 75.8 us -> 69.7 us (0.920)
  Pallas kernels: 19.5 us -> 14.2 us
  waiting for transfers between devices: 19.9 us -> 16 us
  starting transfers between devices: 31.6 us -> 33.8 us
  local copies, waits for them, and re-layouts: 2.37 us -> 3.52 us
    pallas_call x3 -> x8, Pallas kernels: 19.5 us -> 14.2 us  [the longest x2 3.24 us: near_call(): pl.pallas_call(lambda *refs: near_kernel(first, *refs), name='near', comp...]
    ppermute x11 -> x12, waiting for transfers between devices: 19.9 us -> 16 us  [from_partner(): lax.ppermute(value, axis, [(i, i ^ mask) for i in range(lax.axis_size(axi...]
    ppermute x11 -> x12, starting transfers between devices: 26.8 us -> 29.1 us  [from_partner(): lax.ppermute(value, axis, [(i, i ^ mask) for i in range(lax.axis_size(axi...]
    unnamed x27 -> x15, local copies, waits for them, and re-layouts: 2.28 us -> 3.52 us
    ppermute x4 -> x5, starting transfers between devices: 4.83 us -> 4.75 us  [local(): far.append(lax.ppermute(near[k], 'harm', skip))]
    select_n x5 -> x4, other arithmetic: 1.64 us -> 1.71 us  [the longest x3 1.67 us: local(): middle = jnp.where(bit(stage + 1), swapped, middle)]
  transfers between devices with their start and end apart: 15 -> 17, of which waited for: 7 -> 4; matrix products, arithmetic and copies ran while one was open for 3% -> 3% of each run, Pallas kernels for 7% -> 14%
where the time goes in v2:
time: 69.7 us; the launch traced here: 69.4 us
  starting transfers between devices  33.8 us (48%)
  waiting for transfers between devices  16 us (23%)
  Pallas kernels  14.2 us (20%)
  local copies, waits for them, and re-layouts  3.52 us (5%)
  other arithmetic  1.72 us (2%)
    ppermute x12, starting transfers between devices, from_partner(): lax.ppermute(value, axis, [(i, i ^ mask) for i in range(lax.axis_size(axi...  29.1 us
    ppermute x12, waiting for transfers between devices, from_partner(): lax.ppermute(value, axis, [(i, i ^ mask) for i in range(lax.axis_size(axi...  16 us
    ppermute x5, starting transfers between devices, local(): far.append(lax.ppermute(near[k], 'harm', skip))  4.75 us
    unnamed x15, local copies, waits for them, and re-layouts  3.52 us
    pallas_call x2, Pallas kernels, near_call(): pl.pallas_call(lambda *refs: near_kernel(first, *refs), name='near', comp...  3.24 us
    pallas_call x1, Pallas kernels, local(): pl.pallas_call(main_kernel, name='main', compiler_params=KERNEL_MEMORY, i...  2.51 us
    pallas_call x1, Pallas kernels, local(): pl.pallas_call(lift_kernel, name='lift', compiler_params=KERNEL_MEMORY, i...  2.5 us
    pallas_call x1, Pallas kernels, local(): pl.pallas_call(cut_kernel, name='cut', compiler_params=KERNEL_MEMORY, in_...  1.87 us
  transfers between devices with their start and end apart: 17, of which 4 were waited for; matrix products, arithmetic and copies ran while one was open for 3% of the time, Pallas kernels for 14%

profile of v2, /device:TPU:1, one launch (start us, length us, event | category | flops | bytes accessed | tf_op | source)
XLA Modules:
  0.0 69.4 jit_solution(3846941410187931402)
XLA Ops:
  0.0 1.9 %cut.1 = (f32[2,8,64,256]{3,2,1,0:T(8,128)S(1)}, f32[2,2,64,256]{3,2,1,0:T(8,128)S(1)}, f32[2,2,64,256]{3,2,1,0:T(8,128)S(1)}, f32[2,2,64,256]{3,2,1,0:T(8,128)S...) custom-call(f32[2,8,64,256]{3,2,1,0:T(8,128)} %response.1), custom_call_target="tpu_custom_call" | custom-call | tf_op jit(solution)/shard_map/cut/pallas_call | solution.py:361
  1.9 1.6 %traces.1 = (f32[24,16,128]{2,1,0:T(8,128)S(1)}, f32[16,16,128]{2,1,0:T(8,128)S(1)}, f32[8,16,128]{2,1,0:T(8,128)S(1)}, s32[8,128]{1,0:T(8,128)S(1)}) custom-call(s32[4]{0:T(128)} %masks.3, f32[2,8,64,256]{3,2,1,0:T(8,128)S(1)} %get-tuple-element.17.response, f32[4,16,64]{2,1,0:T(8,128)} %trace_mats.1, s32[4,64]{1,0:T(4,128)} %send_elem.1, s32[4,64]{1,0:T(4,128)} %send_face.1), custom_call_target="tpu_custom_call" | custom-call | tf_op jit(solution)/shard_map/traces/pallas_call | solution.py:379
  3.5 3.1 %collective-permute-start.11 = (f32[16,16,128]{2,1,0:T(8,128)S(1)}, f32[16,16,128]{2,1,0:T(8,128)S(1)}, u32[]{:S(2)}, u32[]{:S(2)}) collective-permute-start(f32[16,16,128]{2,1,0:T(8,128)S(1)} %get-tuple-element.26), channel_id=1, source_target_pairs={{0,3},{1,2},{2,1},{3,0},{4,7},{5,6},{6,5},{7,4},{8,11},{9,10},{10,... | collective-permute-start | bytes 393224 | tf_op jit(solution)/shard_map/ppermute | solution.py:337
  6.6 1.5 %collective-permute-start.12 = (f32[16,16,128]{2,1,0:T(8,128)S(1)}, f32[16,16,128]{2,1,0:T(8,128)S(1)}, u32[]{:S(2)}, u32[]{:S(2)}) collective-permute-start(f32[16,16,128]{2,1,0:T(8,128)S(1)} %get-tuple-element.26), channel_id=1, source_target_pairs={{0,2},{1,3},{2,0},{3,1},{4,6},{5,7},{6,4},{7,5},{8,10},{9,11},{10,... | collective-permute-start | bytes 393224 | tf_op jit(solution)/shard_map/ppermute | solution.py:337
  8.1 1.6 %collective-permute-done.11 = f32[16,16,128]{2,1,0:T(8,128)S(1)} collective-permute-done((f32[16,16,128]{2,1,0:T(8,128)S(1)}, f32[16,16,128]{2,1,0:T(8,128)S(1)}, u32[]{:S(2)}, u32[]{:S(2)}) %collective-permute-start.11) | collective-permute-done | bytes 131104 | tf_op jit(solution)/shard_map/ppermute | solution.py:337
  9.7 3.8 %collective-permute-done.12 = f32[16,16,128]{2,1,0:T(8,128)S(1)} collective-permute-done((f32[16,16,128]{2,1,0:T(8,128)S(1)}, f32[16,16,128]{2,1,0:T(8,128)S(1)}, u32[]{:S(2)}, u32[]{:S(2)}) %collective-permute-start.12) | collective-permute-done | bytes 131104 | tf_op jit(solution)/shard_map/ppermute | solution.py:337
  13.5 2.4 %collective-permute-start.13 = (f32[16,16,128]{2,1,0:T(8,128)S(1)}, f32[16,16,128]{2,1,0:T(8,128)S(1)}, u32[]{:S(2)}, u32[]{:S(2)}) collective-permute-start(f32[16,16,128]{2,1,0:T(8,128)S(1)} %fusion), channel_id=1, source_target_pairs={{0,4},{1,5},{2,6},{3,7},{4,0},{5,1},{6,2},{7,3},{8,12},{9,13},{10,... | collective-permute-start | bytes 393224 | tf_op jit(solution)/shard_map/ppermute | solution.py:337
  15.9 1.3 %collective-permute-start = (f32[2,2,64,256]{3,2,1,0:T(8,128)S(1)}, f32[2,2,64,256]{3,2,1,0:T(8,128)}, u32[]{:S(2)}, u32[]{:S(2)}) collective-permute-start(f32[2,2,64,256]{3,2,1,0:T(8,128)S(1)} %get-tuple-element.18), channel_id=1, source_target_pairs={{0,32},{32,0},{64,96},{96,64},{128,160},{160,128},{192,224},{224,1... | collective-permute-start | bytes 786440 | tf_op jit(solution)/shard_map/ppermute | solution.py:337
  17.4 1.3 %collective-permute-start.2 = (f32[2,2,64,256]{3,2,1,0:T(8,128)S(1)}, f32[2,2,64,256]{3,2,1,0:T(8,128)}, u32[]{:S(2)}, u32[]{:S(2)}) collective-permute-start(f32[2,2,64,256]{3,2,1,0:T(8,128)S(1)} %get-tuple-element.20), channel_id=1, source_target_pairs={{0,32},{32,0},{64,96},{96,64},{128,160},{160,128},{192,224},{224,1... | collective-permute-start | bytes 786440 | tf_op jit(solution)/shard_map/ppermute | solution.py:337
  19.0 7.3 %collective-permute-start.14 = (f32[16,16,128]{2,1,0:T(8,128)S(1)}, f32[16,16,128]{2,1,0:T(8,128)S(1)}, u32[]{:S(2)}, u32[]{:S(2)}) collective-permute-start(f32[16,16,128]{2,1,0:T(8,128)S(1)} %broadcast_select_fusion), channel_id=1, source_target_pairs={{0,12},{1,13},{2,14},{3,15},{4,8},{5,9},{6,10},{7,11},{8,4},{9,5},... | collective-permute-start | bytes 393224 | tf_op jit(solution)/shard_map/ppermute | solution.py:337
  26.3 10.5 %collective-permute-done.3.refs_3_ = f32[2,1,64,256]{3,2,1,0:T(8,128)} collective-permute-done((f32[2,1,64,256]{3,2,1,0:T(8,128)S(1)}, f32[2,1,64,256]{3,2,1,0:T(8,128)}, u32[]{:S(2)}, u32[]{:S(2)}) %collective-permute-start.3) | collective-permute-done | bytes 131104 | tf_op jit(solution)/shard_map/ppermute | solution.py:337
  36.8 1.3 %collective-permute-start.4 = (f32[2,1,64,256]{3,2,1,0:T(8,128)S(1)}, f32[2,1,64,256]{3,2,1,0:T(8,128)S(1)}, u32[]{:S(2)}, u32[]{:S(2)}) collective-permute-start(f32[2,1,64,256]{3,2,1,0:T(8,128)S(1)} %get-tuple-element.22), channel_id=1, source_target_pairs={{0,32},{32,0},{64,96},{96,64},{128,160},{160,128},{192,224},{224,1... | collective-permute-start | bytes 393224 | tf_op jit(solution)/shard_map/ppermute | solution.py:337
  38.1 1.2 %collective-permute-start.8 = (f32[2,1,64,256]{3,2,1,0:T(8,128)}, f32[2,1,64,256]{3,2,1,0:T(8,128)}, u32[]{:S(2)}, u32[]{:S(2)}) collective-permute-start(f32[2,1,64,256]{3,2,1,0:T(8,128)} %collective-permute-done.3.refs_3_), channel_id=1, source_target_pairs={{0,64},{32,224},{64,128},{96,32},{128,192},{160,96},{192,0},{224,1... | collective-permute-start | bytes 393224 | tf_op jit(solution)/shard_map/ppermute | solution.py:375
  39.3 1.2 %collective-permute-start.5 = (f32[2,2,64,256]{3,2,1,0:T(8,128)}, f32[2,2,64,256]{3,2,1,0:T(8,128)}, u32[]{:S(2)}, u32[]{:S(2)}) collective-permute-start(f32[2,2,64,256]{3,2,1,0:T(8,128)} %collective-permute-done.refs_2_), channel_id=1, source_target_pairs={{0,64},{32,224},{64,128},{96,32},{128,192},{160,96},{192,0},{224,1... | collective-permute-start | bytes 786440 | tf_op jit(solution)/shard_map/ppermute | solution.py:375
  42.9 2.6 %collective-permute-start.15 = (f32[16,16,128]{2,1,0:T(8,128)}, f32[16,16,128]{2,1,0:T(8,128)}, u32[]{:S(2)}, u32[]{:S(2)}) collective-permute-start(f32[16,16,128]{2,1,0:T(8,128)} %broadcast_select_fusion.1), channel_id=1, source_target_pairs={{0,16},{1,17},{2,18},{3,19},{4,20},{5,21},{6,22},{7,23},{8,24},{9,... | collective-permute-start | bytes 393224 | tf_op jit(solution)/shard_map/ppermute | solution.py:337
  45.5 1.4 %own.1.refs_1_ = f32[2,8,64,256]{3,2,1,0:T(8,128)S(1)} custom-call(f32[2,8,64,256]{3,2,1,0:T(8,128)S(1)} %get-tuple-element.17.response, f32[2,17,64,256]{3,2,1,0:T(8,128)S(1)} %copy-done), custom_call_target="tpu_custom_call" | custom-call | tf_op jit(solution)/shard_map/own/pallas_call | solution.py:405
  48.6 1.2 %copy-done.2 = f32[2,8,64,256]{3,2,1,0:T(8,128)S(1)} copy-done((f32[2,8,64,256]{3,2,1,0:T(8,128)S(1)}, f32[2,8,64,256]{3,2,1,0:T(8,128)}, u32[]{:S(2)}) %copy-start.2) | copy-done | bytes 1048600
  49.8 1.6 %near.2.refs_1_ = f32[2,8,64,256]{3,2,1,0:T(8,128)S(1)} custom-call(f32[2,17,64,256]{3,2,1,0:T(8,128)S(1)} %copy-done, f32[2,8,64,256]{3,2,1,0:T(8,128)S(1)} %copy-done.2, f32[2,2,64,256]{3,2,1,0:T(8,128)} %collective-permute-done.refs_2_, f32[2,2,64,256]{3,2,1,0:T(8,128)} %collective-permute-done.1.refs_3_), custom_call_target="tpu_custom_call" | custom-call | tf_op jit(solution)/shard_map/near/pallas_call | solution.py:415
  51.4 1.7 %near.3.acc = f32[2,8,64,256]{3,2,1,0:T(8,128)S(1)} custom-call(f32[2,17,64,256]{3,2,1,0:T(8,128)S(1)} %copy-done, f32[2,8,64,256]{3,2,1,0:T(8,128)S(1)} %near.2.refs_1_, f32[2,2,64,256]{3,2,1,0:T(8,128)} %collective-permute-done.2.refs_2_, f32[2,1,64,256]{3,2,1,0:T(8,128)} %collective-permute-done.3.refs_3_, f32[2,1,64,256]{3,2,1,0:T(8,128)S(1)} %copy-done.5), custom_call_target="tpu_custom_call" | custom-call | tf_op jit(solution)/shard_map/near/pallas_call | solution.py:415
  53.1 7.9 %collective-permute-start.10 = (f32[8,16,128]{2,1,0:T(8,128)S(1)}, f32[8,16,128]{2,1,0:T(8,128)S(1)}, u32[]{:S(2)}, u32[]{:S(2)}) collective-permute-start(f32[8,16,128]{2,1,0:T(8,128)S(1)} %get-tuple-element.24), channel_id=1, source_target_pairs={{0,31},{1,30},{2,29},{3,28},{4,27},{5,26},{6,25},{7,24},{8,23},{9,... | collective-permute-start | bytes 196616 | tf_op jit(solution)/shard_map/ppermute | solution.py:337
  61.1 1.2 %collective-permute-start.16 = (f32[2,1,64,256]{3,2,1,0:T(8,128)S(1)}, f32[2,1,64,256]{3,2,1,0:T(8,128)S(1)}, u32[]{:S(2)}, u32[]{:S(2)}) collective-permute-start(f32[2,1,64,256]{3,2,1,0:T(8,128)S(1)} %copy-done.5), channel_id=1, source_target_pairs={{0,64},{32,224},{64,128},{96,32},{128,192},{160,96},{192,0},{224,1... | collective-permute-start | bytes 393224 | tf_op jit(solution)/shard_map/ppermute | solution.py:375
  62.3 2.5 %main.1.image = f32[2,8,64,256]{3,2,1,0:T(8,128)S(1)} custom-call(f32[2,17,64,256]{3,2,1,0:T(8,128)S(1)} %copy-done, f32[2,8,64,256]{3,2,1,0:T(8,128)S(1)} %near.3.acc, f32[64,64]{1,0:T(8,128)S(1)} %copy-done.3, f32[2,2,64,256]{3,2,1,0:T(8,128)} %collective-permute-done.5.refs_0_, f32[2,2,64,256]{3,2,1,0:T(8,128)} %collective-permute-done.6.refs_1_, ...), custom_call_target="tpu_custom_call" | custom-call | tf_op jit(solution)/shard_map/main/pallas_call | solution.py:426
  65.8 2.5 %lift.1 = (f32[2,8,64,256]{3,2,1,0:T(8,128)}, f32[2,1,64,256]{3,2,1,0:T(8,128)S(1)}) custom-call(s32[4]{0:T(128)} %masks.3, f32[2,8,64,256]{3,2,1,0:T(8,128)S(1)} %get-tuple-element.17.response, f32[2,8,64,256]{3,2,1,0:T(8,128)S(1)} %main.1.image, f32[64,16]{1,0:T(8,128)} %copy.11.lift_mat, s32[4,64]{1,0:T(4,128)} %recv_elem.1, ...), custom_call_target="tpu_custom_call" | custom-call | tf_op jit(solution)/shard_map/lift/pallas_call | solution.py:437
  68.3 1.1 %tail.1 = f32[2,8,64,256]{3,2,1,0:T(8,128)} custom-call(f32[2,17,64,256]{3,2,1,0:T(8,128)S(1)} %copy-done, f32[64,64]{1,0:T(8,128)S(1)} %copy-done.3, f32[2,1,64,256]{3,2,1,0:T(8,128)S(1)} %get-tuple-element.27.edge, f32[2,1,64,256]{3,2,1,0:T(8,128)S(1)} %collective-permute-done.16.chunk, ...), custom_call_target="tpu_custom_call", output_to_operand_aliasing={{}: (4, {})} | custom-call | tf_op jit(solution)/shard_map/tail/pallas_call | solution.py:446
  (38 shorter events, 5.7 us)
Async XLA Ops:
  0.0 45.5 %copy-start = (f32[2,17,64,256]{3,2,1,0:T(8,128)S(1)}, f32[2,17,64,256]{3,2,1,0:T(8,128)}, u32[]{:S(2)}) copy-start(f32[2,17,64,256]{3,2,1,0:T(8,128)} %coeff.5) | copy-start | bytes 6684676
  3.5 6.2 %collective-permute-start.11 = (f32[16,16,128]{2,1,0:T(8,128)S(1)}, f32[16,16,128]{2,1,0:T(8,128)S(1)}, u32[]{:S(2)}, u32[]{:S(2)}) collective-permute-start(f32[16,16,128]{2,1,0:T(8,128)S(1)} %get-tuple-element.26), channel_id=1, source_target_pairs={{0,3},{1,2},{2,1},{3,0},{4,7},{5,6},{6,5},{7,4},{8,11},{9,10},{10,... | collective-permute-start | bytes 393224 | tf_op jit(solution)/shard_map/ppermute | solution.py:337
  6.6 6.9 %collective-permute-start.12 = (f32[16,16,128]{2,1,0:T(8,128)S(1)}, f32[16,16,128]{2,1,0:T(8,128)S(1)}, u32[]{:S(2)}, u32[]{:S(2)}) collective-permute-start(f32[16,16,128]{2,1,0:T(8,128)S(1)} %get-tuple-element.26), channel_id=1, source_target_pairs={{0,2},{1,3},{2,0},{3,1},{4,6},{5,7},{6,4},{7,5},{8,10},{9,11},{10,... | collective-permute-start | bytes 393224 | tf_op jit(solution)/shard_map/ppermute | solution.py:337
  8.1 5.3 %collective-permute-start.9 = (f32[24,16,128]{2,1,0:T(8,128)S(1)}, f32[24,16,128]{2,1,0:T(8,128)S(1)}, u32[]{:S(2)}, u32[]{:S(2)}) collective-permute-start(f32[24,16,128]{2,1,0:T(8,128)S(1)} %get-tuple-element.23), channel_id=1, source_target_pairs={{0,1},{1,0},{2,3},{3,2},{4,5},{5,4},{6,7},{7,6},{8,9},{9,8},{10,11... | collective-permute-start | bytes 589832 | tf_op jit(solution)/shard_map/ppermute | solution.py:337
  13.5 5.5 %collective-permute-start.13 = (f32[16,16,128]{2,1,0:T(8,128)S(1)}, f32[16,16,128]{2,1,0:T(8,128)S(1)}, u32[]{:S(2)}, u32[]{:S(2)}) collective-permute-start(f32[16,16,128]{2,1,0:T(8,128)S(1)} %fusion), channel_id=1, source_target_pairs={{0,4},{1,5},{2,6},{3,7},{4,0},{5,1},{6,2},{7,3},{8,12},{9,13},{10,... | collective-permute-start | bytes 393224 | tf_op jit(solution)/shard_map/ppermute | solution.py:337
  15.9 22.1 %collective-permute-start = (f32[2,2,64,256]{3,2,1,0:T(8,128)S(1)}, f32[2,2,64,256]{3,2,1,0:T(8,128)}, u32[]{:S(2)}, u32[]{:S(2)}) collective-permute-start(f32[2,2,64,256]{3,2,1,0:T(8,128)S(1)} %get-tuple-element.18), channel_id=1, source_target_pairs={{0,32},{32,0},{64,96},{96,64},{128,160},{160,128},{192,224},{224,1... | collective-permute-start | bytes 786440 | tf_op jit(solution)/shard_map/ppermute | solution.py:337
  17.2 22.1 %collective-permute-start.1 = (f32[2,2,64,256]{3,2,1,0:T(8,128)S(1)}, f32[2,2,64,256]{3,2,1,0:T(8,128)}, u32[]{:S(2)}, u32[]{:S(2)}) collective-permute-start(f32[2,2,64,256]{3,2,1,0:T(8,128)S(1)} %get-tuple-element.19), channel_id=1, source_target_pairs={{0,32},{32,0},{64,96},{96,64},{128,160},{160,128},{192,224},{224,1... | collective-permute-start | bytes 786440 | tf_op jit(solution)/shard_map/ppermute | solution.py:337
  17.4 23.1 %collective-permute-start.2 = (f32[2,2,64,256]{3,2,1,0:T(8,128)S(1)}, f32[2,2,64,256]{3,2,1,0:T(8,128)}, u32[]{:S(2)}, u32[]{:S(2)}) collective-permute-start(f32[2,2,64,256]{3,2,1,0:T(8,128)S(1)} %get-tuple-element.20), channel_id=1, source_target_pairs={{0,32},{32,0},{64,96},{96,64},{128,160},{160,128},{192,224},{224,1... | collective-permute-start | bytes 786440 | tf_op jit(solution)/shard_map/ppermute | solution.py:337
  18.7 18.1 %collective-permute-start.3 = (f32[2,1,64,256]{3,2,1,0:T(8,128)S(1)}, f32[2,1,64,256]{3,2,1,0:T(8,128)}, u32[]{:S(2)}, u32[]{:S(2)}) collective-permute-start(f32[2,1,64,256]{3,2,1,0:T(8,128)S(1)} %get-tuple-element.21), channel_id=1, source_target_pairs={{0,32},{32,0},{64,96},{96,64},{128,160},{160,128},{192,224},{224,1... | collective-permute-start | bytes 393224 | tf_op jit(solution)/shard_map/ppermute | solution.py:337
  19.0 22.4 %collective-permute-start.14 = (f32[16,16,128]{2,1,0:T(8,128)S(1)}, f32[16,16,128]{2,1,0:T(8,128)S(1)}, u32[]{:S(2)}, u32[]{:S(2)}) collective-permute-start(f32[16,16,128]{2,1,0:T(8,128)S(1)} %broadcast_select_fusion), channel_id=1, source_target_pairs={{0,12},{1,13},{2,14},{3,15},{4,8},{5,9},{6,10},{7,11},{8,4},{9,5},... | collective-permute-start | bytes 393224 | tf_op jit(solution)/shard_map/ppermute | solution.py:337
  36.8 5.5 %collective-permute-start.4 = (f32[2,1,64,256]{3,2,1,0:T(8,128)S(1)}, f32[2,1,64,256]{3,2,1,0:T(8,128)S(1)}, u32[]{:S(2)}, u32[]{:S(2)}) collective-permute-start(f32[2,1,64,256]{3,2,1,0:T(8,128)S(1)} %get-tuple-element.22), channel_id=1, source_target_pairs={{0,32},{32,0},{64,96},{96,64},{128,160},{160,128},{192,224},{224,1... | collective-permute-start | bytes 393224 | tf_op jit(solution)/shard_map/ppermute | solution.py:337
  38.1 15.0 %collective-permute-start.8 = (f32[2,1,64,256]{3,2,1,0:T(8,128)}, f32[2,1,64,256]{3,2,1,0:T(8,128)}, u32[]{:S(2)}, u32[]{:S(2)}) collective-permute-start(f32[2,1,64,256]{3,2,1,0:T(8,128)} %collective-permute-done.3.refs_3_), channel_id=1, source_target_pairs={{0,64},{32,224},{64,128},{96,32},{128,192},{160,96},{192,0},{224,1... | collective-permute-start | bytes 393224 | tf_op jit(solution)/shard_map/ppermute | solution.py:375
  39.3 21.8 %collective-permute-start.5 = (f32[2,2,64,256]{3,2,1,0:T(8,128)}, f32[2,2,64,256]{3,2,1,0:T(8,128)}, u32[]{:S(2)}, u32[]{:S(2)}) collective-permute-start(f32[2,2,64,256]{3,2,1,0:T(8,128)} %collective-permute-done.refs_2_), channel_id=1, source_target_pairs={{0,64},{32,224},{64,128},{96,32},{128,192},{160,96},{192,0},{224,1... | collective-permute-start | bytes 786440 | tf_op jit(solution)/shard_map/ppermute | solution.py:375
  40.5 21.8 %collective-permute-start.6 = (f32[2,2,64,256]{3,2,1,0:T(8,128)}, f32[2,2,64,256]{3,2,1,0:T(8,128)}, u32[]{:S(2)}, u32[]{:S(2)}) collective-permute-start(f32[2,2,64,256]{3,2,1,0:T(8,128)} %collective-permute-done.1.refs_3_), channel_id=1, source_target_pairs={{0,64},{32,224},{64,128},{96,32},{128,192},{160,96},{192,0},{224,1... | collective-permute-start | bytes 786440 | tf_op jit(solution)/shard_map/ppermute | solution.py:375
  41.4 20.9 %collective-permute-start.7 = (f32[2,2,64,256]{3,2,1,0:T(8,128)}, f32[2,2,64,256]{3,2,1,0:T(8,128)}, u32[]{:S(2)}, u32[]{:S(2)}) collective-permute-start(f32[2,2,64,256]{3,2,1,0:T(8,128)} %collective-permute-done.2.refs_2_), channel_id=1, source_target_pairs={{0,64},{32,224},{64,128},{96,32},{128,192},{160,96},{192,0},{224,1... | collective-permute-start | bytes 786440 | tf_op jit(solution)/shard_map/ppermute | solution.py:375
  42.3 5.6 %copy-start.6 = (f32[64,16]{0,1:T(8,128)S(1)}, f32[64,16]{0,1:T(8,128)}, u32[]{:S(2)}) copy-start(f32[64,16]{0,1:T(8,128)} %param.13) | copy-start | bytes 12292
  42.3 0.6 copy-start.4
  42.9 21.9 %collective-permute-start.15 = (f32[16,16,128]{2,1,0:T(8,128)}, f32[16,16,128]{2,1,0:T(8,128)}, u32[]{:S(2)}, u32[]{:S(2)}) collective-permute-start(f32[16,16,128]{2,1,0:T(8,128)} %broadcast_select_fusion.1), channel_id=1, source_target_pairs={{0,16},{1,17},{2,18},{3,19},{4,20},{5,21},{6,22},{7,23},{8,24},{9,... | collective-permute-start | bytes 393224 | tf_op jit(solution)/shard_map/ppermute | solution.py:337
  46.9 1.0 %copy-start.1 = (f32[2,8,64,256]{3,2,1,0:T(8,128)}, f32[2,8,64,256]{3,2,1,0:T(8,128)S(1)}, u32[]{:S(2)}) copy-start(f32[2,8,64,256]{3,2,1,0:T(8,128)S(1)} %own.1.refs_1_) | copy-start | bytes 3145732
  48.6 1.2 %copy-start.2 = (f32[2,8,64,256]{3,2,1,0:T(8,128)S(1)}, f32[2,8,64,256]{3,2,1,0:T(8,128)}, u32[]{:S(2)}) copy-start(f32[2,8,64,256]{3,2,1,0:T(8,128)} %copy-done.1) | copy-start | bytes 3145732
  49.8 1.6 %copy-start.5 = (f32[2,1,64,256]{3,2,1,0:T(8,128)S(1)}, f32[2,1,64,256]{3,2,1,0:T(8,128)}, u32[]{:S(2)}) copy-start(f32[2,1,64,256]{3,2,1,0:T(8,128)} %copy-done.4) | copy-start | bytes 393220
  51.4 10.9 %copy-start.3 = (f32[64,64]{1,0:T(8,128)S(1)}, f32[64,64]{1,0:T(8,128)}, u32[]{:S(2)}) copy-start(f32[64,64]{1,0:T(8,128)} %volume_mat.3) | copy-start | bytes 49156
  53.1 12.7 %collective-permute-start.10 = (f32[8,16,128]{2,1,0:T(8,128)S(1)}, f32[8,16,128]{2,1,0:T(8,128)S(1)}, u32[]{:S(2)}, u32[]{:S(2)}) collective-permute-start(f32[8,16,128]{2,1,0:T(8,128)S(1)} %get-tuple-element.24), channel_id=1, source_target_pairs={{0,31},{1,30},{2,29},{3,28},{4,27},{5,26},{6,25},{7,24},{8,23},{9,... | collective-permute-start | bytes 196616 | tf_op jit(solution)/shard_map/ppermute | solution.py:337
  61.1 7.2 %collective-permute-start.16 = (f32[2,1,64,256]{3,2,1,0:T(8,128)S(1)}, f32[2,1,64,256]{3,2,1,0:T(8,128)S(1)}, u32[]{:S(2)}, u32[]{:S(2)}) collective-permute-start(f32[2,1,64,256]{3,2,1,0:T(8,128)S(1)} %copy-done.5), channel_id=1, source_target_pairs={{0,64},{32,224},{64,128},{96,32},{128,192},{160,96},{192,0},{224,1... | collective-permute-start | bytes 393224 | tf_op jit(solution)/shard_map/ppermute | solution.py:375
